TPU v7x, 32 devices: a whole 2x2x4 slice. The times are simulated.
32 devices in a mesh: groups: 2 (over x), cols: 4 (over y, core), rows: 4 (over z).
Axes of the slice: x: 2, y: 2, z: 4, core: 2. Of those that a mesh axis runs over, the one named last changes fastest.
Arguments:
- camera_tokens: bfloat16 [1024, 6144], P(('groups', 'rows'), 'cols'), parts along dimension 0, may hold values from -150 to 150, as said below
- norm_gain: float32 [6144], P('cols'), may hold values from 0.25 to 1.75
- query_weight: bfloat16 [6144, 6144], P('cols', 'rows'), may hold values from -0.078125 to 0.078125
- key_weight: bfloat16 [6144, 6144], P('cols', 'rows'), may hold values from -0.078125 to 0.078125
- value_weight: bfloat16 [6144, 6144], P('cols', 'rows'), may hold values from -0.078125 to 0.078125
- query_gain: float32 [6144], P('rows'), may hold values from 0.5 to 14, as said below
- key_gain: float32 [6144], P('rows'), may hold values from 0.5 to 14, as said below
- out_weight: bfloat16 [6144, 6144], P('rows', 'cols'), may hold values from -0.078125 to 0.078125
- up_weight: bfloat16 [6144, 24576], P('cols', 'rows'), may hold values from -0.078125 to 0.078125
- up_bias: float32 [24576], P('rows'), may hold values from -3 to 3
- down_weight: bfloat16 [24576, 6144], P('rows', 'cols'), may hold values from -0.0390625 to 0.0390625
- down_bias: float32 [6144], P('cols'), may hold values from -3 to 3
- join_gain: float32 [6144], P('cols'), may hold values from 0.25 to 1.75
- join_query: bfloat16 [6144, 6144], P('cols', 'rows'), may hold values from -0.078125 to 0.078125
- join_key: bfloat16 [6144, 6144], P('cols', 'rows'), may hold values from -0.078125 to 0.078125
- join_value: bfloat16 [6144, 6144], P('cols', 'rows'), may hold values from -0.078125 to 0.078125
- join_query_gain: float32 [6144], P('rows'), may hold values from 0.5 to 14, as said below
- join_key_gain: float32 [6144], P('rows'), may hold values from 0.5 to 14, as said below
- join_out: bfloat16 [6144, 6144], P('rows', 'cols'), may hold values from -0.078125 to 0.078125
Outputs:
- joined_tokens: bfloat16 [1024, 6144], P(('groups', 'rows'), 'cols'), parts along dimension 0
There are 2 independent parts, one for each index of `groups`. A program takes and returns all parts, laid end to end along the dimension named above; an argument that names none is the same for every part. Nothing has to cross between parts.
Inputs may be any that keep to these rules, and one draw needn't show every extreme that they name: `camera_tokens`: real valued tokens. `query_gain`: Positive. `key_gain`: Positive. `join_query_gain`: Positive. `join_key_gain`: Positive.
All inputs are finite; a program needn't handle non-finite values.
Results may differ from a plain program's by a relative error of at most 0.012.
Values may be sent and summed in bfloat16 or wider, within the bound.
A program may use at most 192 MiB of HBM per device.

v0:
```python
import math

import jax
import jax.numpy as jnp
from jax import lax
from jax.sharding import PartitionSpec as P

HEAD_DIM = 128
TOK_CAM = 64
D = 6144


EPS = 1e-06


def partner_2(array, axis, bit):
    return lax.ppermute(array, axis, [(i, i ^ 1 << bit) for i in range(lax.axis_size(axis))])


def normalize(values, scales, moments):
    row_mean = moments[0] / D
    row_var = moments[1] / D - row_mean * row_mean
    return ((values - row_mean[:, None]) * lax.rsqrt(row_var[:, None] + EPS) * scales).astype(
        jnp.bfloat16
    )


def shard_moments(values):
    return lax.psum((jnp.sum(values, 1), jnp.sum(values * values, 1)), "cols")


def head_norm(values, scales):
    row_count = values.shape[0]
    grouped = values.reshape(row_count, -1, HEAD_DIM)
    row_mean = jnp.mean(grouped, -1, keepdims=True)
    row_var = jnp.mean(grouped * grouped, -1, keepdims=True) - row_mean * row_mean
    normed = (grouped - row_mean) * lax.rsqrt(row_var + EPS)
    return (normed.reshape(row_count, -1) * scales).astype(jnp.bfloat16)


def attend(queries, key_rows, val_rows):
    inv_root = 1.0 / math.sqrt(HEAD_DIM)
    scores = (
        jnp.einsum("bqhd,bkhd->bhqk", queries, key_rows, preferred_element_type=jnp.float32)
        * inv_root
    )
    row_max = jnp.max(scores, -1, keepdims=True)
    weights = jnp.exp(scores - row_max)
    row_sum = jnp.sum(weights, -1)
    blended = jnp.einsum(
        "bhqk,bkhd->bqhd",
        weights.astype(jnp.bfloat16),
        val_rows,
        preferred_element_type=jnp.float32,
    )
    return blended / jnp.transpose(row_sum, (0, 2, 1))[..., None]


def to_heads(matrix, blocks):
    return matrix.reshape(blocks, -1, matrix.shape[1] // HEAD_DIM, HEAD_DIM)


def camera_attention(queries, key_rows, val_rows):
    local_rows = queries.shape[0]
    if local_rows >= TOK_CAM:
        blocks = local_rows // TOK_CAM
        result = attend(
            to_heads(queries, blocks), to_heads(key_rows, blocks), to_heads(val_rows, blocks)
        )
    else:
        cam_span = TOK_CAM // local_rows
        position = lax.axis_index("cols")
        key_value = jnp.stack((key_rows, val_rows))
        for which_bit in range(cam_span.bit_length() - 1):
            partner = partner_2(key_value, "cols", which_bit)
            is_lower = position >> which_bit & 1 == 0
            key_value = jnp.where(
                is_lower,
                jnp.concatenate((key_value, partner), 1),
                jnp.concatenate((partner, key_value), 1),
            )
        result = attend(to_heads(queries, 1), to_heads(key_value[0], 1), to_heads(key_value[1], 1))
    return result.reshape(local_rows, -1).astype(jnp.bfloat16)


def body(
    camera_tokens,
    norm_gain,
    query_weight,
    key_weight,
    value_weight,
    query_gain,
    key_gain,
    out_weight,
    up_weight,
    up_bias,
    down_weight,
    down_bias,
    join_gain,
    join_query,
    join_key,
    join_value,
    join_query_gain,
    join_key_gain,
    join_out,
):
    own_rows = camera_tokens.shape[0]
    all_rows = own_rows * lax.axis_size("rows")
    col_rows = all_rows // lax.axis_size("cols")
    attn_width = query_weight.shape[1]
    start_f32 = camera_tokens.astype(jnp.float32)
    normed_all = lax.all_gather(
        normalize(start_f32, norm_gain, shard_moments(start_f32)), "rows", axis=0, tiled=True
    )
    joint_weight = jnp.concatenate((query_weight, key_weight, value_weight, up_weight), 1)
    joint = lax.psum_scatter(
        jnp.dot(normed_all, joint_weight, preferred_element_type=jnp.float32),
        "cols",
        scatter_dimension=0,
        tiled=True,
    )
    up_sum = joint[:, 3 * attn_width :]
    hidden = jax.nn.gelu(up_sum + up_bias, approximate=False).astype(jnp.bfloat16)
    attended = camera_attention(
        head_norm(joint[:, :attn_width], query_gain),
        head_norm(joint[:, attn_width : 2 * attn_width], key_gain),
        joint[:, 2 * attn_width : 3 * attn_width].astype(jnp.bfloat16),
    )
    attn_all, hidden_all = (
        lax.all_gather(attended, "cols", axis=0, tiled=True),
        lax.all_gather(hidden, "cols", axis=0, tiled=True),
    )
    mixed = lax.psum_scatter(
        jnp.dot(attn_all, out_weight, preferred_element_type=jnp.float32)
        + jnp.dot(hidden_all, down_weight, preferred_element_type=jnp.float32),
        "rows",
        scatter_dimension=0,
        tiled=True,
    )
    layer_own = (start_f32 + mixed + down_bias).astype(jnp.bfloat16)
    layer_f32 = layer_own.astype(jnp.float32)
    join_in = lax.all_gather(
        normalize(layer_f32, join_gain, shard_moments(layer_f32)), "rows", axis=0, tiled=True
    )
    join_weight = jnp.concatenate((join_query, join_key, join_value), 1)
    join_joint = lax.psum_scatter(
        jnp.dot(join_in, join_weight, preferred_element_type=jnp.float32),
        "cols",
        scatter_dimension=0,
        tiled=True,
    )
    join_q = head_norm(join_joint[:, :attn_width], join_query_gain)
    join_k = head_norm(join_joint[:, attn_width : 2 * attn_width], join_key_gain)
    join_v = join_joint[:, 2 * attn_width :].astype(jnp.bfloat16)
    heads_here = attn_width // HEAD_DIM
    query_heads = join_q.reshape(col_rows, heads_here, HEAD_DIM)
    inv_root = 1.0 / math.sqrt(HEAD_DIM)
    run_max = jnp.full((heads_here, col_rows), -jnp.inf, jnp.float32)
    run_sum = jnp.zeros((heads_here, col_rows), jnp.float32)
    accum = jnp.zeros((col_rows, heads_here, HEAD_DIM), jnp.float32)
    key_part = lax.all_gather(join_k, "cols", axis=0, tiled=True)
    val_part = lax.all_gather(join_v, "cols", axis=0, tiled=True)
    row_count = key_part.shape[0]
    key_heads = key_part.reshape(row_count, heads_here, HEAD_DIM)
    val_heads = val_part.reshape(row_count, heads_here, HEAD_DIM)
    scores = (
        jnp.einsum("qhd,khd->hqk", query_heads, key_heads, preferred_element_type=jnp.float32)
        * inv_root
    )
    new_max = jnp.max(scores, -1)
    factor = jnp.exp(run_max - new_max)
    weights = jnp.exp(scores - new_max[..., None])
    run_sum = run_sum * factor + jnp.sum(weights, -1)
    accum = accum * jnp.transpose(factor)[..., None] + jnp.einsum(
        "hqk,khd->qhd", weights.astype(jnp.bfloat16), val_heads, preferred_element_type=jnp.float32
    )
    run_max, run_sum, accum = (new_max, run_sum, accum)
    joined_attn = (
        (accum / jnp.transpose(run_sum)[..., None])
        .reshape(col_rows, attn_width)
        .astype(jnp.bfloat16)
    )
    joined_all = lax.all_gather(joined_attn, "cols", axis=0, tiled=True)
    result = lax.psum_scatter(
        jnp.dot(joined_all, join_out, preferred_element_type=jnp.float32),
        "rows",
        scatter_dimension=0,
        tiled=True,
    )
    return (layer_own.astype(jnp.float32) + result).astype(jnp.bfloat16)


def solution(mesh):
    in_specs = (
        P(("groups", "rows"), "cols"),
        P("cols"),
        P("cols", "rows"),
        P("cols", "rows"),
        P("cols", "rows"),
        P("rows"),
        P("rows"),
        P("rows", "cols"),
        P("cols", "rows"),
        P("rows"),
        P("rows", "cols"),
        P("cols"),
        P("cols"),
        P("cols", "rows"),
        P("cols", "rows"),
        P("cols", "rows"),
        P("rows"),
        P("rows"),
        P("rows", "cols"),
    )
    out_specs = P(("groups", "rows"), "cols")
    return jax.shard_map(body, mesh=mesh, in_specs=in_specs, out_specs=out_specs, check_vma=False)
```

profile of v0, /device:TPU:0, one launch (start us, length us, event | category | flops | bytes accessed | tf_op | source)
XLA Modules:
  0.0 695.8 jit_solution(5860410591741534853)
XLA Ops:
  6.5 1.2 convert_reduce_fusion.1
  7.7 8.4 %all-reduce.1 = (f32[128]{0:T(128)S(1)}, f32[128]{0:T(128)S(1)}) all-reduce(f32[128]{0:T(128)S(1)} %get-tuple-element.16, f32[128]{0:T(128)S(1)} %get-tuple-element.15), channel_id=1, replica_groups=mesh['groups'=2,'cols'=4,'rows'=4] {'cols'}, use_global_device_ids=true, to_apply=%region_3.0 | all-reduce | flops 256 | bytes 2048 | tf_op jit(solution)/shard_map/psum | solution.py:29
  16.1 2.0 fusion.46
  18.2 37.4 %all-gather.8.cloned.1.call-done = bf16[512,1536]{1,0:T(8,128)(2,1)} async-done(((bf16[128,1536]{1,0:T(8,128)(2,1)}), bf16[512,1536]{1,0:T(8,128)(2,1)}) %all-gather.8.cloned.1.call-update) | async-done | bytes 1572880 | tf_op jit(solution)/shard_map/all_gather | solution.py:112
  55.7 35.7 %fusion = f32[512,10752]{1,0:T(8,128)} fusion(bf16[512,1536]{1,0:T(8,128)(2,1)} %all-gather.8.cloned.1.call-done, bf16[1536,6144]{1,0:T(8,128)(2,1)} %param.27, bf16[1536,1536]{1,0:T(8,128)(2,1)} %param.23, bf16[1536,1536]{1,0:T(8,128)(2,1)} %param.22, bf16[1536,1536]{1,0:T(8,128)(2,1)} %param.21), kind=kOutput, calls=%fused_computation | convolution fusion | flops 17043554304 | bytes 56623104 | tf_op jit(solution)/shard_map/dot_general | solution.py:117
  91.4 155.8 %reduce-scatter.5.cloned.1.call-done = f32[128,10752]{1,0:T(8,128)} async-done(((f32[512,10752]{1,0:T(8,128)}), f32[128,10752]{1,0:T(8,128)}) %reduce-scatter.5.cloned.1.call-update) | async-done | bytes 5505040 | tf_op jit(solution)/shard_map/reduce_scatter | solution.py:116
  249.5 1.5 fusion.70
  254.0 2.1 multiply_convert_fusion.3
  258.9 8.8 %fusion.16 = bf16[128,6144]{1,0:T(8,128)(2,1)} fusion(f32[128,10752]{1,0:T(8,128)} %reduce-scatter.5.cloned.1.call-done, f32[6144]{0:T(1024)S(1)} %copy-done.3), kind=kLoop, calls=%fused_computation.18 | loop fusion | flops 51904512 | bytes 4743168 | tf_op jit(solution)/shard_map/convert_element_type | solution.py:123
  267.9 10.7 %all-gather.10.cloned.1.call-done = bf16[512,1536]{1,0:T(8,128)(2,1)} async-done(((bf16[128,1536]{1,0:T(8,128)(2,1)}), bf16[512,1536]{1,0:T(8,128)(2,1)}) %all-gather.10.cloned.1.call-update) | async-done | bytes 1572880 | tf_op jit(solution)/shard_map/all_gather | solution.py:130
  278.6 4.9 fusion.73
  283.5 42.9 %all-gather.12.cloned.1.call-done = bf16[512,6144]{1,0:T(8,128)(2,1)} async-done(((bf16[128,6144]{1,0:T(8,128)(2,1)}), bf16[512,6144]{1,0:T(8,128)(2,1)}) %all-gather.12.cloned.1.call-update) | async-done | bytes 6291472 | tf_op jit(solution)/shard_map/all_gather | solution.py:131
  326.4 16.8 %convolution_add_fusion = f32[512,1536]{1,0:T(8,128)} fusion(f32[512,1536]{1,0:T(8,128)S(1)} %fusion.73, bf16[512,6144]{1,0:T(8,128)(2,1)} %all-gather.12.cloned.1.call-done, bf16[6144,1536]{1,0:T(8,128)(2,1)} %param.29), kind=kOutput, calls=%fused_computation.15 | convolution fusion | flops 9664462848 | bytes 31457280 | tf_op jit(solution)/shard_map/dot_general | solution.py:135
  343.3 60.5 %reduce-scatter.7.cloned.1.call-done = f32[128,1536]{1,0:T(8,128)} async-done(((f32[512,1536]{1,0:T(8,128)}), f32[128,1536]{1,0:T(8,128)}) %reduce-scatter.7.cloned.1.call-update) | async-done | bytes 786448 | tf_op jit(solution)/shard_map/reduce_scatter | solution.py:133
  403.8 1.4 convert_reduce_fusion
  405.2 6.2 all-reduce
  412.5 36.8 %all-gather.14.cloned.1.call-done = bf16[512,1536]{1,0:T(8,128)(2,1)} async-done(((bf16[128,1536]{1,0:T(8,128)(2,1)}), bf16[512,1536]{1,0:T(8,128)(2,1)}) %all-gather.14.cloned.1.call-update) | async-done | bytes 1572880 | tf_op jit(solution)/shard_map/all_gather | solution.py:142
  449.3 16.6 %fusion.8 = f32[512,4608]{1,0:T(8,128)} fusion(bf16[512,1536]{1,0:T(8,128)(2,1)} %all-gather.14.cloned.1.call-done, bf16[1536,1536]{1,0:T(8,128)(2,1)} %param.34, bf16[1536,1536]{1,0:T(8,128)(2,1)} %param.33, bf16[1536,1536]{1,0:T(8,128)(2,1)} %param.32), kind=kOutput, calls=%fused_computation.8 | convolution fusion | flops 7290224640 | bytes 25165824 | tf_op jit(solution)/shard_map/dot_general | solution.py:147
  466.0 76.9 %reduce-scatter.9.cloned.1.call-done = f32[128,4608]{1,0:T(8,128)} async-done(((f32[512,4608]{1,0:T(8,128)}), f32[128,4608]{1,0:T(8,128)}) %reduce-scatter.9.cloned.1.call-update) | async-done | bytes 2359312 | tf_op jit(solution)/shard_map/reduce_scatter | solution.py:146
  542.9 1.5 fusion.71
  546.4 1.2 copy.43
  550.0 2.9 multiply_convert_fusion
  555.1 17.7 %all-gather.16.cloned.1.call-done = bf16[512,1536]{1,0:T(8,128)(2,1)} async-done(((bf16[128,1536]{1,0:T(8,128)(2,1)}), bf16[512,1536]{1,0:T(8,128)(2,1)}) %all-gather.16.cloned.1.call-update) | async-done | bytes 1572880 | tf_op jit(solution)/shard_map/all_gather | solution.py:161
  572.8 2.6 copy.45
  575.4 2.2 multiply_reduce_fusion
  579.2 14.9 %all-gather.18.cloned.1.call-done = bf16[512,1536]{1,0:T(8,128)(2,1)} async-done(((bf16[128,1536]{1,0:T(8,128)(2,1)}), bf16[512,1536]{1,0:T(8,128)(2,1)}) %all-gather.18.cloned.1.call-update) | async-done | bytes 1572880 | tf_op jit(solution)/shard_map/all_gather | solution.py:162
  594.1 2.6 copy.48
  596.7 2.9 fusion.41
  599.7 19.9 %all-gather.20.cloned.1.call-done = bf16[512,1536]{0,1:T(8,128)(2,1)} async-done(((bf16[128,1536]{0,1:T(8,128)(2,1)}), bf16[512,1536]{0,1:T(8,128)(2,1)}) %all-gather.20.cloned.1.call-update) | async-done | bytes 1572880 | tf_op jit(solution)/shard_map/all_gather | solution.py:183
  619.6 7.1 %fusion.74 = f32[512,1536]{1,0:T(8,128)} fusion(bf16[512,1536]{0,1:T(8,128)(2,1)} %all-gather.20.cloned.1.call-done, bf16[1536,1536]{1,0:T(8,128)(2,1)} %param.37), kind=kOutput, calls=%fused_computation.112 | convolution fusion | flops 2415919104 | bytes 9437184 | tf_op jit(solution)/shard_map/dot_general | solution.py:185
  626.7 60.6 %reduce-scatter.11.cloned.1.call-done = f32[128,1536]{1,0:T(8,128)} async-done(((f32[512,1536]{1,0:T(8,128)}), f32[128,1536]{1,0:T(8,128)}) %reduce-scatter.11.cloned.1.call-update) | async-done | bytes 786448 | tf_op jit(solution)/shard_map/reduce_scatter | solution.py:184
  687.3 1.9 fusion.54
  (83 shorter events, 17.6 us)
Async XLA Ops:
  6.5 49.1 %all-gather.8.cloned.1.call-start = ((), (), s32[]{:S(2)}) async-start(), calls=%async_computation.4 | async-start | bytes 1966080 | tf_op jit(solution)/shard_map/all_gather | solution.py:112
  18.2 229.1 %reduce-scatter.5.cloned.1.call-start = ((), (), s32[]{:S(2)}) async-start(), calls=%async_computation.5 | async-start | bytes 27525120 | tf_op jit(solution)/shard_map/reduce_scatter | solution.py:116
  91.4 187.2 %all-gather.10.cloned.1.call-start = ((), (), s32[]{:S(2)}) async-start(), calls=%async_computation.6 | async-start | bytes 1966080 | tf_op jit(solution)/shard_map/all_gather | solution.py:130
  252.3 1.7 copy-start.4
  252.3 1.7 copy-start.5
  256.1 1.1 copy-start.2
  257.2 1.7 copy-start.3
  258.8 67.6 %all-gather.12.cloned.1.call-start = ((), (), s32[]{:S(2)}) async-start(), calls=%async_computation.7 | async-start | bytes 7864320 | tf_op jit(solution)/shard_map/all_gather | solution.py:131
  267.7 136.2 %reduce-scatter.7.cloned.1.call-start = ((), (), s32[]{:S(2)}) async-start(), calls=%async_computation.8 | async-start | bytes 3932160 | tf_op jit(solution)/shard_map/reduce_scatter | solution.py:133
  343.3 60.6 %copy-start.1 = (bf16[128,1536]{1,0:T(8,128)(2,1)S(1)}, bf16[128,1536]{1,0:T(8,128)(2,1)}, u32[]{:S(2)}) copy-start(bf16[128,1536]{1,0:T(8,128)(2,1)} %param.19) | copy-start | bytes 1179652
  343.3 60.6 %copy-start.6 = (f32[1536]{0:T(1024)S(1)}, f32[1536]{0:T(1024)}, u32[]{:S(2)}) copy-start(f32[1536]{0:T(1024)} %param.30) | copy-start | bytes 18436
  343.3 68.1 %copy-start.7 = (f32[1536]{0:T(1024)S(1)}, f32[1536]{0:T(1024)}, u32[]{:S(2)}) copy-start(f32[1536]{0:T(1024)} %param.31) | copy-start | bytes 18436
  343.3 106.0 %all-gather.14.cloned.1.call-start = ((), (), s32[]{:S(2)}) async-start(), calls=%async_computation.9 | async-start | bytes 1966080 | tf_op jit(solution)/shard_map/all_gather | solution.py:142
  412.5 130.4 %reduce-scatter.9.cloned.1.call-start = ((), (), s32[]{:S(2)}) async-start(), calls=%async_computation.10 | async-start | bytes 11796480 | tf_op jit(solution)/shard_map/reduce_scatter | solution.py:146
  465.9 106.9 %all-gather.16.cloned.1.call-start = ((), (), s32[]{:S(2)}) async-start(), calls=%async_computation.11 | async-start | bytes 1966080 | tf_op jit(solution)/shard_map/all_gather | solution.py:161
  546.4 3.6 copy-start
  547.7 2.4 copy-start.8
  553.0 41.1 %all-gather.18.cloned.1.call-start = ((), (), s32[]{:S(2)}) async-start(), calls=%async_computation.12 | async-start | bytes 1966080 | tf_op jit(solution)/shard_map/all_gather | solution.py:162
  553.9 65.7 %all-gather.20.cloned.1.call-start = ((), (), s32[]{:S(2)}) async-start(), calls=%async_computation.13 | async-start | bytes 1966080 | tf_op jit(solution)/shard_map/all_gather | solution.py:183
  599.6 87.7 %reduce-scatter.11.cloned.1.call-start = ((), (), s32[]{:S(2)}) async-start(), calls=%async_computation.14 | async-start | bytes 3932160 | tf_op jit(solution)/shard_map/reduce_scatter | solution.py:184
Sparse Core Ops, SparseCore 0:
  18.3 37.3 all-gather.7
  91.5 155.6 reduce-scatter.4
  258.9 19.6 all-gather.9
  280.0 46.3 all-gather.11
  343.4 60.3 reduce-scatter.6
  412.6 36.6 all-gather.13
  466.1 76.7 reduce-scatter.8
  553.1 19.6 all-gather.15
  574.4 19.6 all-gather.17
  599.7 19.8 all-gather.19
  626.9 60.3 reduce-scatter.10
where the time goes:
time: 696 us
  waiting for transfers between devices  534 us (77%)
  matrix products  87.2 us (13%)
  other arithmetic  23.5 us (3%)
  local copies, waits for them, and re-layouts  21.9 us (3%)
  blocking collectives  14.6 us (2%)
  between operations  13.5 us (2%)
    reduce_scatter x1, waiting for transfers between devices, body(): lax.psum_scatter(jnp.dot(normed_all, joint_weight, preferred_element_type...  156 us
    reduce_scatter x1, waiting for transfers between devices, body(): lax.psum_scatter(jnp.dot(join_in, join_weight, preferred_element_type=jnp...  76.9 us
    reduce_scatter x1, waiting for transfers between devices, body(): lax.psum_scatter(jnp.dot(joined_all, join_out, preferred_element_type=jnp...  60.6 us
    reduce_scatter x1, waiting for transfers between devices, body(): lax.psum_scatter(jnp.dot(attn_all, out_weight, preferred_element_type=jnp...  60.5 us
    all_gather x1, waiting for transfers between devices, body(): lax.all_gather(hidden, 'cols', axis=0, tiled=True)  42.9 us
    all_gather x1, waiting for transfers between devices, body(): lax.all_gather(normalize(start_f32, norm_gain, shard_moments(start_f32)),...  37.4 us
    all_gather x1, waiting for transfers between devices, body(): lax.all_gather(normalize(layer_f32, join_gain, shard_moments(layer_f32)),...  36.8 us
    dot_general x1, matrix products, body(): jnp.dot(normed_all, joint_weight, preferred_element_type=jnp.float32)  35.7 us
  transfers between devices with their start and end apart: 11, of which 11 were waited for; matrix products, arithmetic and copies ran while one was open for 3% of the time, Pallas kernels for 0%

commit v1 on v0

--- a/solution.py
+++ b/solution.py
@@ -1,8 +1,11 @@
+import functools
 import math
 
 import jax
 import jax.numpy as jnp
 from jax import lax
+from jax.experimental import pallas as pl
+from jax.experimental.pallas import tpu as pltpu
 from jax.sharding import PartitionSpec as P
 
 HEAD_DIM = 128
@@ -83,7 +86,7 @@
     return result.reshape(local_rows, -1).astype(jnp.bfloat16)
 
 
-def body(
+def plain_body(
     camera_tokens,
     norm_gain,
     query_weight,
@@ -190,6 +193,619 @@
     return (layer_own.astype(jnp.float32) + result).astype(jnp.bfloat16)
 
 
+F32 = jnp.float32
+BF16 = jnp.bfloat16
+MESH = pl.DeviceIdType.MESH
+VMEM_LIMIT = 66 * 1024 * 1024 - 3 * 1024 * 1024
+
+
+def each(count, step):
+    lax.fori_loop(0, count, lambda i, carry: (step(i), carry)[1], None)
+
+
+def remote(src, dst, send, recv, device):
+    return pltpu.make_async_remote_copy(
+        src_ref=src,
+        dst_ref=dst,
+        send_sem=send,
+        recv_sem=recv,
+        device_id=device,
+        device_id_type=MESH,
+    )
+
+
+def places():
+    col = lax.axis_index("cols")
+    core = lax.rem(col, 2)
+    return col, col + 1 - 2 * core, lax.rem(col + 2, 4)
+
+
+def greet(cols_away):
+    col, row, row_count = lax.axis_index("cols"), lax.axis_index("rows"), lax.axis_size("rows")
+    barrier = pltpu.get_barrier_semaphore()
+    _, mate, across = places()
+    others = {1: mate, 2: across}
+    if cols_away == 3:
+        others[3] = mate + across - col
+    for other in others.values():
+        pl.semaphore_signal(barrier, inc=1, device_id={"cols": other}, device_id_type=MESH)
+
+    @pl.when(row > 0)
+    def _():
+        pl.semaphore_signal(barrier, inc=1, device_id={"rows": row - 1}, device_id_type=MESH)
+
+    @pl.when(row < row_count - 1)
+    def _():
+        pl.semaphore_signal(barrier, inc=1, device_id={"rows": row + 1}, device_id_type=MESH)
+
+    inner = (row > 0) & (row < row_count - 1)
+
+    @pl.when(inner)
+    def _():
+        pl.semaphore_wait(barrier, len(others) + 2)
+
+    @pl.when(jnp.logical_not(inner))
+    def _():
+        pl.semaphore_wait(barrier, len(others) + 1)
+
+
+def gather_rows(normed, send_r, send_l, arrive):
+    row, row_count = lax.axis_index("rows"), lax.axis_size("rows")
+
+    def to_right(block):
+        return remote(
+            normed.at[block], normed.at[block], send_r.at[block], arrive.at[block], {"rows": row + 1}
+        )
+
+    def to_left(block):
+        return remote(
+            normed.at[block], normed.at[block], send_l.at[block], arrive.at[block], {"rows": row - 1}
+        )
+
+    def pass_on(from_left, block):
+        if from_left:
+
+            @pl.when(row < row_count - 1)
+            def _():
+                to_right(block).start()
+        else:
+
+            @pl.when(row > 0)
+            def _():
+                to_left(block).start()
+
+    pass_on(True, row)
+    pass_on(False, row)
+    for away in range(1, row_count):
+
+        @pl.when(row >= away)
+        def _():
+            to_right(row - away).wait_recv()
+            pass_on(True, row - away)
+
+        @pl.when(row + away < row_count)
+        def _():
+            to_left(row + away).wait_recv()
+            pass_on(False, row + away)
+
+    def finish():
+        for block in range(row_count):
+
+            @pl.when((row >= block) & (row < row_count - 1))
+            def _():
+                to_right(block).wait_send()
+
+            @pl.when((row <= block) & (row > 0))
+            def _():
+                to_left(block).wait_send()
+
+    return finish
+
+
+def norm_heads(values, scales):
+    parts = []
+    for start in range(0, values.shape[1], HEAD_DIM):
+        part = values[:, start : start + HEAD_DIM]
+        mean = jnp.mean(part, -1, keepdims=True)
+        var = jnp.mean(part * part, -1, keepdims=True) - mean * mean
+        parts.append((part - mean) * lax.rsqrt(var + EPS))
+    return (jnp.concatenate(parts, 1) * scales).astype(BF16)
+
+
+def soft_blend(query, keys, values):
+    scores = lax.dot_general(
+        query, keys, (((1,), (1,)), ((), ())), preferred_element_type=F32
+    ) * (1.0 / math.sqrt(HEAD_DIM))
+    weights = jnp.exp(scores - jnp.max(scores, -1, keepdims=True))
+    total = jnp.sum(weights, -1, keepdims=True)
+    blended = jnp.dot(weights.astype(BF16), values, preferred_element_type=F32)
+    return (blended / total).astype(BF16)
+
+
+def in_kernel(span, has_up, width, *refs):
+    refs = list(refs)
+    tokens, gain, q_gain, k_gain, wq, wk, wv = refs[:7]
+    refs = refs[7:]
+    if has_up:
+        bias, w_up = refs[:2]
+        refs = refs[2:]
+    out_a = refs.pop(0)
+    if has_up:
+        out_u = refs.pop(0)
+    normed, moments, m_send, m_recv, z_right, z_left, z_arrive, queries, keys, values = refs[:10]
+    groups = [refs[10:21]]
+    if has_up:
+        groups.append(refs[21:32])
+    col, mate, across = places()
+    diagonal = mate + across - col
+    row, row_count = lax.axis_index("rows"), lax.axis_size("rows")
+    own_rows = tokens.shape[0]
+
+    def load(group, unit, owner, source, start):
+        held = group[0]
+        columns = pl.ds(pl.multiple_of(start, HEAD_DIM), held.shape[-1])
+        return pltpu.make_async_copy(
+            source.at[:, columns], held.at[unit * 4 + owner], group[6].at[unit * 4 + owner]
+        )
+
+    def loads(group_id, unit, owner, which=None):
+        group = groups[group_id]
+        wide = group[0].shape[-1]
+        if group_id == 0:
+            return load(group, unit, owner, (wq, wk, wv)[which], owner * wide)
+        return load(group, unit, owner, w_up, owner * (groups[1][5].shape[0] * wide) + unit * wide)
+
+    def start_loads(owner):
+        for which in range(3):
+            loads(0, which, owner, which).start()
+        if has_up:
+            each(groups[1][5].shape[0], lambda unit: loads(1, unit, owner).start())
+
+    order = (diagonal, across, mate, col)
+    for owner in order:
+        start_loads(owner)
+    greet(3)
+
+    own = tokens[...].astype(F32)
+    lane = lax.broadcasted_iota(jnp.int32, (own_rows, HEAD_DIM), 1)
+    mine = jnp.where(
+        lane < HEAD_DIM // 2,
+        jnp.sum(own, 1, keepdims=True),
+        jnp.sum(own * own, 1, keepdims=True),
+    )
+    moments[3] = mine
+    swaps = []
+    for slot, other in enumerate((mate, across, diagonal)):
+        swap = remote(
+            moments.at[3], moments.at[slot], m_send.at[slot], m_recv.at[slot], {"cols": other}
+        )
+        swap.start()
+        swaps.append(swap)
+    for swap in swaps:
+        swap.wait_recv()
+    total = (moments[3] + moments[0]) + (moments[1] + moments[2])
+    mean = total[:, :1] / width
+    var = total[:, HEAD_DIM // 2 : HEAD_DIM // 2 + 1] / width - mean * mean
+    normed[row] = ((own - mean) * lax.rsqrt(var + EPS) * gain[...]).astype(BF16)
+    finish_rows = gather_rows(normed, z_right, z_left, z_arrive)
+    for swap in swaps:
+        swap.wait_send()
+
+    def ops(group):
+        held, p_send, p_recv, y_send, y_recv, own_sum, _, ps, pr, ys, yr = group
+
+        def product(unit, owner):
+            weight = held.at[unit * 4 + owner]
+            pltpu.make_async_copy(weight, weight, group[6].at[unit * 4 + owner]).wait()
+            left = normed[...].reshape(row_count * own_rows, normed.shape[-1])
+            return jnp.dot(left, weight[...], preferred_element_type=F32)
+
+        def to_mate(half, unit):
+            return remote(
+                p_send.at[half, unit],
+                p_recv.at[half, unit],
+                ps.at[half, unit],
+                pr.at[half, unit],
+                {"cols": mate},
+            )
+
+        def to_across(unit):
+            return remote(
+                y_send.at[unit], y_recv.at[unit], ys.at[unit], yr.at[unit], {"cols": across}
+            )
+
+        def first(unit):
+            p_send[0, unit] = product(unit, diagonal).astype(BF16)
+            to_mate(0, unit).start()
+            partial = product(unit, across)
+            to_mate(0, unit).wait_recv()
+            y_send[unit] = (partial + p_recv[0, unit].astype(F32)).astype(BF16)
+            to_across(unit).start()
+
+        def second(unit):
+            p_send[1, unit] = product(unit, mate).astype(BF16)
+            to_mate(1, unit).start()
+            partial = product(unit, col)
+            to_mate(1, unit).wait_recv()
+            own_sum[unit] = partial + p_recv[1, unit].astype(F32)
+
+        def final(unit):
+            to_across(unit).wait_recv()
+            return own_sum[unit] + y_recv[unit].astype(F32)
+
+        def finish(unit):
+            to_mate(0, unit).wait_send()
+            to_mate(1, unit).wait_send()
+            to_across(unit).wait_send()
+
+        return first, second, final, finish, own_sum.shape[0]
+
+    all_ops = [ops(group) for group in groups]
+    for first, second, final, finish, count in all_ops:
+        each(count, first)
+    for first, second, final, finish, count in all_ops:
+        each(count, second)
+    final = all_ops[0][2]
+    wide = groups[0][0].shape[-1]
+    mine = pl.ds(pl.multiple_of(col * wide, HEAD_DIM), wide)
+    queries[...] = norm_heads(final(0), q_gain[:, mine])
+    keys[...] = norm_heads(final(1), k_gain[:, mine])
+    values[...] = final(2).astype(BF16)
+
+    def camera(which):
+        rows = pl.ds(pl.multiple_of(which * span, span), span)
+        for start in range(0, wide, HEAD_DIM):
+            head = slice(start, start + HEAD_DIM)
+            out_a[rows, head] = soft_blend(queries[rows, head], keys[rows, head], values[rows, head])
+
+    each(out_a.shape[0] // span, camera)
+    if has_up:
+        final = all_ops[1][2]
+
+        def activate(unit):
+            raw = final(unit) + bias[col * out_u.shape[0] + unit]
+            out_u[unit] = (raw * (1.0 + lax.erf(raw * math.sqrt(0.5))) * 0.5).astype(BF16)
+
+        each(out_u.shape[0], activate)
+    for first, second, final, finish, count in all_ops:
+        each(count, finish)
+    finish_rows()
+
+
+def in_call(name, number, span, tokens, gain, q_gain, k_gain, weights, up=None):
+    own_rows, depth = tokens.shape
+    all_rows = own_rows * lax.axis_size("rows")
+    cols = lax.axis_size("cols")
+    wide = weights[0].shape[1] // cols
+    groups = [(3, wide)]
+    operands = [tokens, gain[None], q_gain[None], k_gain[None], *weights]
+    any_spec, vmem_spec = pl.BlockSpec(memory_space=pl.ANY), pl.BlockSpec(memory_space=pltpu.VMEM)
+    in_specs = [vmem_spec] * 4 + [any_spec] * 3
+    out_shape = [jax.ShapeDtypeStruct((all_rows, wide), BF16)]
+    if up is not None:
+        up_bias, up_weight = up
+        up_wide = up_tile(up_weight.shape[1] // cols)
+        count = up_weight.shape[1] // cols // up_wide
+        groups.append((count, up_wide))
+        operands += [up_bias.reshape(cols * count, 1, up_wide), up_weight]
+        in_specs += [vmem_spec, any_spec]
+        out_shape.append(jax.ShapeDtypeStruct((count, all_rows, up_wide), BF16))
+    dma = pltpu.SemaphoreType.DMA
+    row_count = lax.axis_size("rows")
+    scratch = [
+        pltpu.VMEM((row_count, own_rows, depth), BF16),
+        pltpu.VMEM((4, own_rows, HEAD_DIM), F32),
+        dma((3,)),
+        dma((3,)),
+        dma((row_count,)),
+        dma((row_count,)),
+        dma((row_count,)),
+    ] + [pltpu.VMEM((all_rows, wide), BF16)] * 3
+    for count, piece in groups:
+        scratch += [
+            pltpu.VMEM((count * 4, depth, piece), BF16),
+            pltpu.VMEM((2, count, all_rows, piece), BF16),
+            pltpu.VMEM((2, count, all_rows, piece), BF16),
+            pltpu.VMEM((count, all_rows, piece), BF16),
+            pltpu.VMEM((count, all_rows, piece), BF16),
+            pltpu.VMEM((count, all_rows, piece), F32),
+            dma((count * 4,)),
+            dma((2, count)),
+            dma((2, count)),
+            dma((count,)),
+            dma((count,)),
+        ]
+    return pl.pallas_call(
+        functools.partial(in_kernel, span, up is not None, float(depth * cols)),
+        name=name,
+        out_shape=out_shape,
+        in_specs=in_specs,
+        out_specs=[vmem_spec] * len(out_shape),
+        scratch_shapes=scratch,
+        compiler_params=pltpu.CompilerParams(
+            collective_id=number, has_side_effects=True, vmem_limit_bytes=VMEM_LIMIT
+        ),
+    )(*operands)
+
+
+def out_kernel(has_up, *refs):
+    refs = list(refs)
+    base, heads, w_out = refs[:3]
+    refs = refs[3:]
+    if has_up:
+        bias, hidden, w_down = refs[:3]
+        refs = refs[3:]
+    result, accum, right_send, left_send, from_left, from_right = refs[:6]
+    r_send, r_recv, l_send, l_recv = refs[6:10]
+    groups = [refs[10:18]]
+    if has_up:
+        groups.append(refs[18:26])
+    col, mate, across = places()
+    diagonal = mate + across - col
+    row, row_count = lax.axis_index("rows"), lax.axis_size("rows")
+    own_rows = base.shape[0]
+    owners = (col, mate, across, diagonal)
+    sources = [(heads, w_out)]
+    if has_up:
+        sources.append((hidden, w_down))
+
+    def load(group_id, unit, place):
+        held, sem = groups[group_id][0], groups[group_id][1]
+        source = sources[group_id][1]
+        deep = held.shape[1]
+        count = held.shape[0] // 4
+        start = pl.multiple_of((owners[place] * count + unit) * deep, HEAD_DIM)
+        return pltpu.make_async_copy(
+            source.at[pl.ds(start, deep)], held.at[place * count + unit], sem.at[place * count + unit]
+        )
+
+    for place in range(4):
+        for group_id, group in enumerate(groups):
+            each(group[0].shape[0] // 4, lambda unit: load(group_id, unit, place).start())
+    greet(2)
+
+    def copies(group_id):
+        _, _, got, y_send, p_send, f_send, y_recv, p_recv = groups[group_id]
+        source = sources[group_id][0]
+
+        def to_across(unit):
+            return remote(
+                source.at[unit], got.at[1, unit], y_send.at[unit], y_recv.at[unit], {"cols": across}
+            )
+
+        def to_mate(unit):
+            return remote(
+                source.at[unit], got.at[0, unit], p_send.at[unit], p_recv.at[0, unit], {"cols": mate}
+            )
+
+        def forward(unit):
+            return remote(
+                got.at[1, unit], got.at[2, unit], f_send.at[unit], p_recv.at[1, unit], {"cols": mate}
+            )
+
+        return to_across, to_mate, forward
+
+    moves = [copies(group_id) for group_id in range(len(groups))]
+    for group_id, (to_across, to_mate, forward) in enumerate(moves):
+        count = groups[group_id][0].shape[0] // 4
+        each(count, lambda unit: to_across(unit).start())
+    for group_id, (to_across, to_mate, forward) in enumerate(moves):
+        count = groups[group_id][0].shape[0] // 4
+        each(count, lambda unit: to_mate(unit).start())
+    accum[...] = jnp.zeros_like(accum)
+
+    def add(group_id, unit, place, piece):
+        load(group_id, unit, place).wait()
+        held = groups[group_id][0]
+        count = held.shape[0] // 4
+        accum[...] += jnp.dot(piece, held[place * count + unit], preferred_element_type=F32)
+
+    for group_id, (to_across, to_mate, forward) in enumerate(moves):
+        count = groups[group_id][0].shape[0] // 4
+        source, got = sources[group_id][0], groups[group_id][2]
+        each(count, lambda unit: add(group_id, unit, 0, source[unit]))
+
+        def from_mate(unit):
+            to_mate(unit).wait_recv()
+            add(group_id, unit, 1, got[0, unit])
+
+        each(count, from_mate)
+
+    for group_id, (to_across, to_mate, forward) in enumerate(moves):
+        count = groups[group_id][0].shape[0] // 4
+        got = groups[group_id][2]
+
+        def from_across(unit):
+            to_across(unit).wait_recv()
+            forward(unit).start()
+            add(group_id, unit, 2, got[1, unit])
+            forward(unit).wait_recv()
+            add(group_id, unit, 3, got[2, unit])
+
+        each(count, from_across)
+
+    def rows_of(block):
+        return accum[pl.ds(pl.multiple_of(block * own_rows, own_rows), own_rows)]
+
+    def to_right(block):
+        return remote(
+            right_send.at[block], from_left.at[block], r_send.at[block], r_recv.at[block], {"rows": row + 1}
+        )
+
+    def to_left(block):
+        return remote(
+            left_send.at[block], from_right.at[block], l_send.at[block], l_recv.at[block], {"rows": row - 1}
+        )
+
+    def run_right(block):
+        @pl.when((row < block) & (row == 0))
+        def _():
+            right_send[block] = rows_of(block).astype(BF16)
+
+        @pl.when((row < block) & (row > 0))
+        def _():
+            to_right(block).wait_recv()
+            right_send[block] = (rows_of(block) + from_left[block].astype(F32)).astype(BF16)
+
+        @pl.when(row < block)
+        def _():
+            to_right(block).start()
+
+    def run_left(block):
+        @pl.when((row > block) & (row == row_count - 1))
+        def _():
+            left_send[block] = rows_of(block).astype(BF16)
+
+        @pl.when((row > block) & (row < row_count - 1))
+        def _():
+            to_left(block).wait_recv()
+            left_send[block] = (rows_of(block) + from_right[block].astype(F32)).astype(BF16)
+
+        @pl.when(row > block)
+        def _():
+            to_left(block).start()
+
+    for step in range(row_count - 1):
+        run_right(row_count - 1 - step)
+        run_left(step)
+
+    for block in range(row_count):
+
+        @pl.when(row == block)
+        def _():
+            total = rows_of(block)
+            if block > 0:
+                to_right(block).wait_recv()
+                total += from_left[block].astype(F32)
+            if block < row_count - 1:
+                to_left(block).wait_recv()
+                total += from_right[block].astype(F32)
+            total += base[...].astype(F32)
+            if has_up:
+                total += bias[...]
+            result[...] = total.astype(BF16)
+
+    for block in range(row_count):
+
+        @pl.when(row < block)
+        def _():
+            to_right(block).wait_send()
+
+        @pl.when(row > block)
+        def _():
+            to_left(block).wait_send()
+
+    for group_id, (to_across, to_mate, forward) in enumerate(moves):
+
+        def finish(unit):
+            to_across(unit).wait_send()
+            to_mate(unit).wait_send()
+            forward(unit).wait_send()
+
+        each(groups[group_id][0].shape[0] // 4, finish)
+
+
+def out_call(name, number, base, heads, w_out, up=None):
+    own_rows, width = base.shape
+    all_rows, wide = heads.shape
+    row_count = lax.axis_size("rows")
+    any_spec, vmem_spec = pl.BlockSpec(memory_space=pl.ANY), pl.BlockSpec(memory_space=pltpu.VMEM)
+    operands = [base, heads[None], w_out]
+    in_specs = [vmem_spec, vmem_spec, any_spec]
+    groups = [(1, wide)]
+    if up is not None:
+        bias, hidden, w_down = up
+        operands += [bias[None], hidden, w_down]
+        in_specs += [vmem_spec, vmem_spec, any_spec]
+        groups.append((hidden.shape[0], hidden.shape[2]))
+    dma = pltpu.SemaphoreType.DMA
+    block = pltpu.VMEM((row_count, own_rows, width), BF16)
+    scratch = [pltpu.VMEM((all_rows, width), F32)] + [block] * 4 + [dma((row_count,))] * 4
+    for count, piece in groups:
+        scratch += [
+            pltpu.VMEM((4 * count, piece, width), BF16),
+            dma((4 * count,)),
+            pltpu.VMEM((3, count, all_rows, piece), BF16),
+            dma((count,)),
+            dma((count,)),
+            dma((count,)),
+            dma((count,)),
+            dma((2, count)),
+        ]
+    return pl.pallas_call(
+        functools.partial(out_kernel, up is not None),
+        name=name,
+        out_shape=jax.ShapeDtypeStruct((own_rows, width), BF16),
+        in_specs=in_specs,
+        out_specs=vmem_spec,
+        scratch_shapes=scratch,
+        compiler_params=pltpu.CompilerParams(
+            collective_id=number, has_side_effects=True, vmem_limit_bytes=VMEM_LIMIT
+        ),
+    )(*operands)
+
+
+def up_tile(columns):
+    for tile in (4 * HEAD_DIM, 2 * HEAD_DIM, HEAD_DIM):
+        if columns % tile == 0:
+            return tile
+    return columns
+
+
+def kernel_body(
+    camera_tokens,
+    norm_gain,
+    query_weight,
+    key_weight,
+    value_weight,
+    query_gain,
+    key_gain,
+    out_weight,
+    up_weight,
+    up_bias,
+    down_weight,
+    down_bias,
+    join_gain,
+    join_query,
+    join_key,
+    join_value,
+    join_query_gain,
+    join_key_gain,
+    join_out,
+):
+    all_rows = camera_tokens.shape[0] * lax.axis_size("rows")
+    heads, hidden = in_call(
+        "camera_in",
+        0,
+        TOK_CAM,
+        camera_tokens,
+        norm_gain,
+        query_gain,
+        key_gain,
+        (query_weight, key_weight, value_weight),
+        (up_bias, up_weight),
+    )
+    layer_own = out_call(
+        "camera_out", 1, camera_tokens, heads, out_weight, (down_bias, hidden, down_weight)
+    )
+    (joined,) = in_call(
+        "join_in",
+        2,
+        all_rows,
+        layer_own,
+        join_gain,
+        join_query_gain,
+        join_key_gain,
+        (join_query, join_key, join_value),
+    )
+    return out_call("join_out", 3, layer_own, joined, join_out)
+
+
+def fits(mesh):
+    cols, rows = mesh.shape["cols"], mesh.shape["rows"]
+    return cols == 4 and rows > 1 and D % (rows * cols * HEAD_DIM) == 0
+
+
 def solution(mesh):
     in_specs = (
         P(("groups", "rows"), "cols"),
@@ -213,4 +829,5 @@
         P("rows", "cols"),
     )
     out_specs = P(("groups", "rows"), "cols")
+    body = kernel_body if fits(mesh) else plain_body
     return jax.shard_map(body, mesh=mesh, in_specs=in_specs, out_specs=out_specs, check_vma=False)

time: 696 us -> 331 us (0.48)
  waiting for transfers between devices: 534 us -> 0 us
  Pallas kernels: 0 us -> 323 us
  matrix products: 87.2 us -> 0 us
  other arithmetic: 23.5 us -> 0 us
  blocking collectives: 14.6 us -> 0 us
  local copies, waits for them, and re-layouts: 21.9 us -> 8.06 us
  between operations: 13.5 us -> 0.06 us
    reduce_scatter x4 -> x0, waiting for transfers between devices: 354 us -> none  [the longest x1 156 us: body(): lax.psum_scatter(jnp.dot(normed_all, joint_weight, preferred_element_type...]
    pallas_call x0 -> x4, Pallas kernels: none -> 323 us  [the longest x2 174 us: in_call(): pl.pallas_call(functools.partial(in_kernel, span, up is not None, float(d...]
    all_gather x7 -> x0, waiting for transfers between devices: 180 us -> none  [the longest x1 42.9 us: body(): lax.all_gather(hidden, 'cols', axis=0, tiled=True)]
    dot_general x9 -> x0, matrix products: 87.2 us -> none  [the longest x1 35.7 us: body(): jnp.dot(normed_all, joint_weight, preferred_element_type=jnp.float32)]
    convert_element_type x6 -> x0, other arithmetic: 18.8 us -> none  [the longest x1 8.8 us: body(): jax.nn.gelu(up_sum + up_bias, approximate=False).astype(jnp.bfloat16)]
    psum x2 -> x0, blocking collectives: 14.6 us -> none  [shard_moments(): return lax.psum((jnp.sum(values, 1), jnp.sum(values * values, 1)), 'cols')]
  transfers between devices with their start and end apart: 11 -> 0, of which waited for: 11 -> 0; matrix products, arithmetic and copies ran while one was open for 3% -> 0% of each run, Pallas kernels for 0% -> 0%
where the time goes in v1:
time: 331 us
  Pallas kernels  323 us (98%)
  local copies, waits for them, and re-layouts  8.06 us (2%)
    pallas_call x2, Pallas kernels, in_call(): pl.pallas_call(functools.partial(in_kernel, span, up is not None, float(d...  174 us
    pallas_call x2, Pallas kernels, out_call(): pl.pallas_call(functools.partial(out_kernel, up is not None), name=name,...  149 us

profile of v1, /device:TPU:0, one launch (start us, length us, event | category | flops | bytes accessed | tf_op | source)
XLA Modules:
  0.0 331.1 jit_solution(7746383253385969488)
XLA Ops:
  0.0 1.3 broadcast_in_dim.27.refs_1_
  1.3 1.3 broadcast_in_dim.28.refs_2_
  2.6 1.3 broadcast_in_dim.29.refs_3_
  3.9 0.0 copy-start
  3.9 106.0 %camera_in.1 = (bf16[512,384]{1,0:T(8,128)(2,1)}, bf16[3,512,512]{2,1,0:T(8,128)(2,1)}) custom-call(bf16[128,1536]{1,0:T(8,128)(2,1)} %refs_0_.3, f32[1,1536]{1,0:T(1,128)} %broadcast_in_dim.27.refs_1_, f32[1,1536]{1,0:T(1,128)} %broadcast_in_dim.28.refs_2_, f32[1,1536]{1,0:T(1,128)} %broadcast_in_dim.29.refs_3_, bf16[1536,1536]{1,0:T(8,128)(2,1)} %refs_4_.2, ...), custom_call_target="tpu_custom_call" | custom-call | tf_op jit(solution)/shard_map/camera_in/pallas_call | solution.py:518
  109.9 0.0 copy-done
  109.9 0.6 broadcast_in_dim.31.refs_3_
  110.5 0.0 copy-start.1
  110.5 0.0 copy-start.2
  110.5 0.0 copy-start.3
  110.5 91.7 %camera_out.1.refs_0_ = bf16[128,1536]{1,0:T(8,128)(2,1)} custom-call(bf16[128,1536]{1,0:T(8,128)(2,1)} %refs_0_.3, bf16[1,512,384]{2,1,0:T(8,128)(2,1)} %bitcast.4, bf16[1536,1536]{1,0:T(8,128)(2,1)} %refs_2_.2, f32[1,1536]{1,0:T(1,128)} %broadcast_in_dim.31.refs_3_, bf16[3,512,512]{2,1,0:T(8,128)(2,1)} %get-tuple-element.8.refs_4_, bf16[6144,1536]{1,0:T(8,128)(2,1)} %refs_5_.4), custom_call_target="tpu_custom_call" | custom-call | tf_op jit(solution)/shard_map/camera_out/pallas_call | solution.py:735
  202.2 0.0 copy-done.1
  202.2 0.6 broadcast_in_dim.32.refs_1_
  202.8 0.0 copy-done.2
  202.8 0.6 broadcast_in_dim.33.refs_2_
  203.4 0.0 copy-done.3
  203.4 0.6 broadcast_in_dim.34.refs_3_
  204.0 68.5 %join_in.1 = bf16[512,384]{1,0:T(8,128)(2,1)} custom-call(bf16[128,1536]{1,0:T(8,128)(2,1)} %camera_out.1.refs_0_, f32[1,1536]{1,0:T(1,128)} %broadcast_in_dim.32.refs_1_, f32[1,1536]{1,0:T(1,128)} %broadcast_in_dim.33.refs_2_, f32[1,1536]{1,0:T(1,128)} %broadcast_in_dim.34.refs_3_, bf16[1536,1536]{1,0:T(8,128)(2,1)} %refs_4_.3, bf16[1536,1536]{1,0:T(8,128)(2,1)} %refs_5_.5, ...), custom_call_target="tpu_custom_call" | custom-call | tf_op jit(solution)/shard_map/join_in/pallas_call | solution.py:518
  272.4 56.9 %join_out.1 = bf16[128,1536]{1,0:T(8,128)(2,1)} custom-call(bf16[128,1536]{1,0:T(8,128)(2,1)} %camera_out.1.refs_0_, bf16[1,512,384]{2,1,0:T(8,128)(2,1)} %bitcast.3, bf16[1536,1536]{1,0:T(8,128)(2,1)} %refs_2_.3), custom_call_target="tpu_custom_call" | custom-call | tf_op jit(solution)/shard_map/join_out/pallas_call | solution.py:735
  329.3 1.8 copy.21
Async XLA Ops:
  3.9 106.0 %copy-start = (f32[1536]{0:T(1024)S(1)}, f32[1536]{0:T(1024)}, u32[]{:S(2)}) copy-start(f32[1536]{0:T(1024)} %param.30) | copy-start | bytes 18436
  110.5 91.7 %copy-start.1 = (f32[1536]{0:T(1024)S(1)}, f32[1536]{0:T(1024)}, u32[]{:S(2)}) copy-start(f32[1536]{0:T(1024)} %param.31) | copy-start | bytes 18436
  110.5 92.3 %copy-start.2 = (f32[1536]{0:T(1024)S(1)}, f32[1536]{0:T(1024)}, u32[]{:S(2)}) copy-start(f32[1536]{0:T(1024)} %param.35) | copy-start | bytes 18436
  110.5 92.9 %copy-start.3 = (f32[1536]{0:T(1024)S(1)}, f32[1536]{0:T(1024)}, u32[]{:S(2)}) copy-start(f32[1536]{0:T(1024)} %param.36) | copy-start | bytes 18436

commit v2 on v1

--- a/solution.py
+++ b/solution.py
@@ -276,8 +276,8 @@
 
     pass_on(True, row)
     pass_on(False, row)
-    for away in range(1, row_count):
-
+
+    def take(away):
         @pl.when(row >= away)
         def _():
             to_right(row - away).wait_recv()
@@ -299,7 +299,7 @@
             def _():
                 to_left(block).wait_send()
 
-    return finish
+    return take, finish
 
 
 def norm_heads(values, scales):
@@ -340,6 +340,7 @@
     diagonal = mate + across - col
     row, row_count = lax.axis_index("rows"), lax.axis_size("rows")
     own_rows = tokens.shape[0]
+    near = row_count // 2
 
     def load(group, unit, owner, source, start):
         held = group[0]
@@ -386,85 +387,116 @@
     total = (moments[3] + moments[0]) + (moments[1] + moments[2])
     mean = total[:, :1] / width
     var = total[:, HEAD_DIM // 2 : HEAD_DIM // 2 + 1] / width - mean * mean
-    normed[row] = ((own - mean) * lax.rsqrt(var + EPS) * gain[...]).astype(BF16)
-    finish_rows = gather_rows(normed, z_right, z_left, z_arrive)
+    normed[row] = ((own - mean) * lax.rsqrt(var + EPS) * gain[...].reshape(1, -1)).astype(BF16)
+    take_rows, finish_rows = gather_rows(normed, z_right, z_left, z_arrive)
     for swap in swaps:
         swap.wait_send()
 
     def ops(group):
         held, p_send, p_recv, y_send, y_recv, own_sum, _, ps, pr, ys, yr = group
 
-        def product(unit, owner):
+        def product(unit, half, owner, fresh):
             weight = held.at[unit * 4 + owner]
-            pltpu.make_async_copy(weight, weight, group[6].at[unit * 4 + owner]).wait()
-            left = normed[...].reshape(row_count * own_rows, normed.shape[-1])
+            if fresh:
+                pltpu.make_async_copy(weight, weight, group[6].at[unit * 4 + owner]).wait()
+            left = normed[pl.ds(half * near, near)].reshape(near * own_rows, normed.shape[-1])
             return jnp.dot(left, weight[...], preferred_element_type=F32)
 
-        def to_mate(half, unit):
+        def to_mate(kind, unit, half):
             return remote(
-                p_send.at[half, unit],
-                p_recv.at[half, unit],
-                ps.at[half, unit],
-                pr.at[half, unit],
+                p_send.at[kind, unit, half],
+                p_recv.at[kind, unit, half],
+                ps.at[kind, unit, half],
+                pr.at[kind, unit, half],
                 {"cols": mate},
             )
 
-        def to_across(unit):
+        def to_across(unit, half):
             return remote(
-                y_send.at[unit], y_recv.at[unit], ys.at[unit], yr.at[unit], {"cols": across}
+                y_send.at[unit, half],
+                y_recv.at[unit, half],
+                ys.at[unit, half],
+                yr.at[unit, half],
+                {"cols": across},
             )
 
-        def first(unit):
-            p_send[0, unit] = product(unit, diagonal).astype(BF16)
-            to_mate(0, unit).start()
-            partial = product(unit, across)
-            to_mate(0, unit).wait_recv()
-            y_send[unit] = (partial + p_recv[0, unit].astype(F32)).astype(BF16)
-            to_across(unit).start()
-
-        def second(unit):
-            p_send[1, unit] = product(unit, mate).astype(BF16)
-            to_mate(1, unit).start()
-            partial = product(unit, col)
-            to_mate(1, unit).wait_recv()
-            own_sum[unit] = partial + p_recv[1, unit].astype(F32)
-
-        def final(unit):
-            to_across(unit).wait_recv()
-            return own_sum[unit] + y_recv[unit].astype(F32)
+        def first(unit, half, fresh):
+            p_send[0, unit, half] = product(unit, half, diagonal, fresh).astype(BF16)
+            to_mate(0, unit, half).start()
+            partial = product(unit, half, across, fresh)
+            to_mate(0, unit, half).wait_recv()
+            y_send[unit, half] = (partial + p_recv[0, unit, half].astype(F32)).astype(BF16)
+            to_across(unit, half).start()
+
+        def second(unit, half, fresh):
+            p_send[1, unit, half] = product(unit, half, mate, fresh).astype(BF16)
+            to_mate(1, unit, half).start()
+            partial = product(unit, half, col, fresh)
+            to_mate(1, unit, half).wait_recv()
+            own_sum[unit, half] = partial + p_recv[1, unit, half].astype(F32)
+
+        def final(unit, half):
+            to_across(unit, half).wait_recv()
+            return own_sum[unit, half] + y_recv[unit, half].astype(F32)
 
         def finish(unit):
-            to_mate(0, unit).wait_send()
-            to_mate(1, unit).wait_send()
-            to_across(unit).wait_send()
+            for half in range(2):
+                to_mate(0, unit, half).wait_send()
+                to_mate(1, unit, half).wait_send()
+                to_across(unit, half).wait_send()
 
         return first, second, final, finish, own_sum.shape[0]
 
     all_ops = [ops(group) for group in groups]
-    for first, second, final, finish, count in all_ops:
-        each(count, first)
-    for first, second, final, finish, count in all_ops:
-        each(count, second)
+    for away in range(1, near):
+        take_rows(away)
+    home = row // near
+    for half, fresh in ((home, True), (1 - home, False)):
+        for first, second, final, finish, count in all_ops:
+            each(count, lambda unit: first(unit, half, fresh))
+        if fresh:
+            for away in range(near, row_count - 1):
+                take_rows(away)
+        for first, second, final, finish, count in all_ops:
+            each(count, lambda unit: second(unit, half, fresh))
+        if fresh:
+            take_rows(row_count - 1)
     final = all_ops[0][2]
     wide = groups[0][0].shape[-1]
     mine = pl.ds(pl.multiple_of(col * wide, HEAD_DIM), wide)
-    queries[...] = norm_heads(final(0), q_gain[:, mine])
-    keys[...] = norm_heads(final(1), k_gain[:, mine])
-    values[...] = final(2).astype(BF16)
+    half_rows = near * own_rows
+    for half in range(2):
+        rows = slice(half * half_rows, (half + 1) * half_rows)
+        queries[rows] = norm_heads(final(0, half), q_gain[mine].reshape(1, -1))
+        keys[rows] = norm_heads(final(1, half), k_gain[mine].reshape(1, -1))
+        values[rows] = final(2, half).astype(BF16)
 
     def camera(which):
         rows = pl.ds(pl.multiple_of(which * span, span), span)
+        local = pl.ds(pl.multiple_of(lax.rem(which * span, half_rows), span), span)
         for start in range(0, wide, HEAD_DIM):
             head = slice(start, start + HEAD_DIM)
-            out_a[rows, head] = soft_blend(queries[rows, head], keys[rows, head], values[rows, head])
-
-    each(out_a.shape[0] // span, camera)
+            out_a[which * span // half_rows, local, head] = soft_blend(
+                queries[rows, head], keys[rows, head], values[rows, head]
+            )
+
+    def joint(half):
+        for start in range(0, wide, HEAD_DIM):
+            head = slice(start, start + HEAD_DIM)
+            rows = pl.ds(pl.multiple_of(half * half_rows, half_rows), half_rows)
+            out_a[half, :, head] = soft_blend(queries[rows, head], keys[:, head], values[:, head])
+
+    if span == 2 * half_rows:
+        each(2, joint)
+    else:
+        each(2 * half_rows // span, camera)
     if has_up:
         final = all_ops[1][2]
 
         def activate(unit):
-            raw = final(unit) + bias[col * out_u.shape[0] + unit]
-            out_u[unit] = (raw * (1.0 + lax.erf(raw * math.sqrt(0.5))) * 0.5).astype(BF16)
+            for half in range(2):
+                raw = final(unit, half) + bias[col * out_u.shape[0] + unit]
+                out_u[unit, half] = (raw * (1.0 + lax.erf(raw * math.sqrt(0.5))) * 0.5).astype(BF16)
 
         each(out_u.shape[0], activate)
     for first, second, final, finish, count in all_ops:
@@ -478,10 +510,11 @@
     cols = lax.axis_size("cols")
     wide = weights[0].shape[1] // cols
     groups = [(3, wide)]
-    operands = [tokens, gain[None], q_gain[None], k_gain[None], *weights]
+    operands = [tokens, gain, q_gain, k_gain, *weights]
     any_spec, vmem_spec = pl.BlockSpec(memory_space=pl.ANY), pl.BlockSpec(memory_space=pltpu.VMEM)
     in_specs = [vmem_spec] * 4 + [any_spec] * 3
-    out_shape = [jax.ShapeDtypeStruct((all_rows, wide), BF16)]
+    half_rows = all_rows // 2
+    out_shape = [jax.ShapeDtypeStruct((2, half_rows, wide), BF16)]
     if up is not None:
         up_bias, up_weight = up
         up_wide = up_tile(up_weight.shape[1] // cols)
@@ -489,7 +522,7 @@
         groups.append((count, up_wide))
         operands += [up_bias.reshape(cols * count, 1, up_wide), up_weight]
         in_specs += [vmem_spec, any_spec]
-        out_shape.append(jax.ShapeDtypeStruct((count, all_rows, up_wide), BF16))
+        out_shape.append(jax.ShapeDtypeStruct((count, 2, half_rows, up_wide), BF16))
     dma = pltpu.SemaphoreType.DMA
     row_count = lax.axis_size("rows")
     scratch = [
@@ -504,16 +537,16 @@
     for count, piece in groups:
         scratch += [
             pltpu.VMEM((count * 4, depth, piece), BF16),
-            pltpu.VMEM((2, count, all_rows, piece), BF16),
-            pltpu.VMEM((2, count, all_rows, piece), BF16),
-            pltpu.VMEM((count, all_rows, piece), BF16),
-            pltpu.VMEM((count, all_rows, piece), BF16),
-            pltpu.VMEM((count, all_rows, piece), F32),
+            pltpu.VMEM((2, count, 2, half_rows, piece), BF16),
+            pltpu.VMEM((2, count, 2, half_rows, piece), BF16),
+            pltpu.VMEM((count, 2, half_rows, piece), BF16),
+            pltpu.VMEM((count, 2, half_rows, piece), BF16),
+            pltpu.VMEM((count, 2, half_rows, piece), F32),
             dma((count * 4,)),
-            dma((2, count)),
-            dma((2, count)),
-            dma((count,)),
-            dma((count,)),
+            dma((2, count, 2)),
+            dma((2, count, 2)),
+            dma((count, 2)),
+            dma((count, 2)),
         ]
     return pl.pallas_call(
         functools.partial(in_kernel, span, up is not None, float(depth * cols)),
@@ -544,6 +577,7 @@
     diagonal = mate + across - col
     row, row_count = lax.axis_index("rows"), lax.axis_size("rows")
     own_rows = base.shape[0]
+    near = row_count // 2
     owners = (col, mate, across, diagonal)
     sources = [(heads, w_out)]
     if has_up:
@@ -568,64 +602,83 @@
         _, _, got, y_send, p_send, f_send, y_recv, p_recv = groups[group_id]
         source = sources[group_id][0]
 
-        def to_across(unit):
+        def to_across(unit, half):
             return remote(
-                source.at[unit], got.at[1, unit], y_send.at[unit], y_recv.at[unit], {"cols": across}
+                source.at[unit, half],
+                got.at[1, unit, half],
+                y_send.at[unit, half],
+                y_recv.at[unit, half],
+                {"cols": across},
             )
 
-        def to_mate(unit):
+        def to_mate(unit, half):
             return remote(
-                source.at[unit], got.at[0, unit], p_send.at[unit], p_recv.at[0, unit], {"cols": mate}
+                source.at[unit, half],
+                got.at[0, unit, half],
+                p_send.at[unit, half],
+                p_recv.at[0, unit, half],
+                {"cols": mate},
             )
 
-        def forward(unit):
+        def forward(unit, half):
             return remote(
-                got.at[1, unit], got.at[2, unit], f_send.at[unit], p_recv.at[1, unit], {"cols": mate}
+                got.at[1, unit, half],
+                got.at[2, unit, half],
+                f_send.at[unit, half],
+                p_recv.at[1, unit, half],
+                {"cols": mate},
             )
 
-        return to_across, to_mate, forward
+        return to_across, to_mate, forward, groups[group_id][0].shape[0] // 4
 
     moves = [copies(group_id) for group_id in range(len(groups))]
-    for group_id, (to_across, to_mate, forward) in enumerate(moves):
-        count = groups[group_id][0].shape[0] // 4
-        each(count, lambda unit: to_across(unit).start())
-    for group_id, (to_across, to_mate, forward) in enumerate(moves):
-        count = groups[group_id][0].shape[0] // 4
-        each(count, lambda unit: to_mate(unit).start())
-    accum[...] = jnp.zeros_like(accum)
-
-    def add(group_id, unit, place, piece):
-        load(group_id, unit, place).wait()
+    home = row // near
+    halves = ((1 - home, True), (home, False))
+    for half, _ in halves:
+        for to_across, to_mate, forward, count in moves:
+            each(count, lambda unit: to_across(unit, half).start())
+            each(count, lambda unit: to_mate(unit, half).start())
+
+    def add(group_id, unit, place, half, fresh, piece, begin=False):
+        if fresh:
+            load(group_id, unit, place).wait()
         held = groups[group_id][0]
         count = held.shape[0] // 4
-        accum[...] += jnp.dot(piece, held[place * count + unit], preferred_element_type=F32)
-
-    for group_id, (to_across, to_mate, forward) in enumerate(moves):
-        count = groups[group_id][0].shape[0] // 4
-        source, got = sources[group_id][0], groups[group_id][2]
-        each(count, lambda unit: add(group_id, unit, 0, source[unit]))
-
-        def from_mate(unit):
-            to_mate(unit).wait_recv()
-            add(group_id, unit, 1, got[0, unit])
-
-        each(count, from_mate)
-
-    for group_id, (to_across, to_mate, forward) in enumerate(moves):
-        count = groups[group_id][0].shape[0] // 4
-        got = groups[group_id][2]
-
-        def from_across(unit):
-            to_across(unit).wait_recv()
-            forward(unit).start()
-            add(group_id, unit, 2, got[1, unit])
-            forward(unit).wait_recv()
-            add(group_id, unit, 3, got[2, unit])
-
-        each(count, from_across)
+        part = jnp.dot(piece, held[place * count + unit], preferred_element_type=F32)
+        if begin:
+            accum[half] = part
+        else:
+            accum[half] += part
+
+    def near_chunks(half, fresh):
+        for group_id, (to_across, to_mate, forward, count) in enumerate(moves):
+            source, got = sources[group_id][0], groups[group_id][2]
+            if group_id == 0:
+                add(0, 0, 0, half, fresh, source[0, half], True)
+            else:
+                each(count, lambda unit: add(group_id, unit, 0, half, fresh, source[unit, half]))
+
+            def from_mate(unit):
+                to_mate(unit, half).wait_recv()
+                add(group_id, unit, 1, half, fresh, got[0, unit, half])
+
+            each(count, from_mate)
+
+    def far_chunks(half, fresh):
+        for group_id, (to_across, to_mate, forward, count) in enumerate(moves):
+            got = groups[group_id][2]
+
+            def from_across(unit):
+                to_across(unit, half).wait_recv()
+                forward(unit, half).start()
+                add(group_id, unit, 2, half, fresh, got[1, unit, half])
+                forward(unit, half).wait_recv()
+                add(group_id, unit, 3, half, fresh, got[2, unit, half])
+
+            each(count, from_across)
 
     def rows_of(block):
-        return accum[pl.ds(pl.multiple_of(block * own_rows, own_rows), own_rows)]
+        return accum[block // near, (block % near) * own_rows : (block % near + 1) * own_rows]
 
     def to_right(block):
         return remote(
@@ -665,9 +718,37 @@
         def _():
             to_left(block).start()
 
+    def send_far(from_end):
+        at_end = (row == 0) | (row == row_count - 1)
+        now = at_end if from_end else jnp.logical_not(at_end)
+        for step in range(near):
+
+            @pl.when(now & (row < near))
+            def _():
+                run_right(row_count - 1 - step)
+
+            @pl.when(now & (row >= near))
+            def _():
+                run_left(step)
+
+    near_chunks(*halves[0])
+    far_chunks(*halves[0])
+    send_far(True)
+    near_chunks(*halves[1])
+    send_far(False)
+    far_chunks(*halves[1])
     for step in range(row_count - 1):
-        run_right(row_count - 1 - step)
-        run_left(step)
+        block = row_count - 1 - step
+
+        @pl.when(home == block // near)
+        def _():
+            run_right(block)
+
+    for block in range(row_count - 1):
+
+        @pl.when(home == block // near)
+        def _():
+            run_left(block)
 
     for block in range(row_count):
 
@@ -682,7 +763,7 @@
                 total += from_right[block].astype(F32)
             total += base[...].astype(F32)
             if has_up:
-                total += bias[...]
+                total += bias[...].reshape(1, -1)
             result[...] = total.astype(BF16)
 
     for block in range(row_count):
@@ -695,19 +776,20 @@
         def _():
             to_left(block).wait_send()
 
-    for group_id, (to_across, to_mate, forward) in enumerate(moves):
+    for to_across, to_mate, forward, count in moves:
 
         def finish(unit):
-            to_across(unit).wait_send()
-            to_mate(unit).wait_send()
-            forward(unit).wait_send()
-
-        each(groups[group_id][0].shape[0] // 4, finish)
+            for half in range(2):
+                to_across(unit, half).wait_send()
+                to_mate(unit, half).wait_send()
+                forward(unit, half).wait_send()
+
+        each(count, finish)
 
 
 def out_call(name, number, base, heads, w_out, up=None):
     own_rows, width = base.shape
-    all_rows, wide = heads.shape
+    _, half_rows, wide = heads.shape
     row_count = lax.axis_size("rows")
     any_spec, vmem_spec = pl.BlockSpec(memory_space=pl.ANY), pl.BlockSpec(memory_space=pltpu.VMEM)
     operands = [base, heads[None], w_out]
@@ -715,22 +797,22 @@
     groups = [(1, wide)]
     if up is not None:
         bias, hidden, w_down = up
-        operands += [bias[None], hidden, w_down]
+        operands += [bias, hidden, w_down]
         in_specs += [vmem_spec, vmem_spec, any_spec]
-        groups.append((hidden.shape[0], hidden.shape[2]))
+        groups.append((hidden.shape[0], hidden.shape[3]))
     dma = pltpu.SemaphoreType.DMA
     block = pltpu.VMEM((row_count, own_rows, width), BF16)
-    scratch = [pltpu.VMEM((all_rows, width), F32)] + [block] * 4 + [dma((row_count,))] * 4
+    scratch = [pltpu.VMEM((2, half_rows, width), F32)] + [block] * 4 + [dma((row_count,))] * 4
     for count, piece in groups:
         scratch += [
             pltpu.VMEM((4 * count, piece, width), BF16),
             dma((4 * count,)),
-            pltpu.VMEM((3, count, all_rows, piece), BF16),
-            dma((count,)),
-            dma((count,)),
-            dma((count,)),
-            dma((count,)),
-            dma((2, count)),
+            pltpu.VMEM((3, count, 2, half_rows, piece), BF16),
+            dma((count, 2)),
+            dma((count, 2)),
+            dma((count, 2)),
+            dma((count, 2)),
+            dma((2, count, 2)),
         ]
     return pl.pallas_call(
         functools.partial(out_kernel, up is not None),
@@ -803,7 +885,7 @@
 
 def fits(mesh):
     cols, rows = mesh.shape["cols"], mesh.shape["rows"]
-    return cols == 4 and rows > 1 and D % (rows * cols * HEAD_DIM) == 0
+    return cols == 4 and rows > 2 and rows % 2 == 0 and D % (rows * cols * HEAD_DIM) == 0
 
 
 def solution(mesh):

time: 331 us -> 258 us (0.78)
  Pallas kernels: 323 us -> 256 us
  local copies, waits for them, and re-layouts: 8.06 us -> 1.77 us
    pallas_call x2, Pallas kernels: 149 us -> 111 us  [out_call(): pl.pallas_call(functools.partial(out_kernel, up is not None), name=name,...]
    pallas_call x2, Pallas kernels: 174 us -> 145 us  [in_call(): pl.pallas_call(functools.partial(in_kernel, span, up is not None, float(d...]
    broadcast_in_dim x7 -> x0, local copies, waits for them, and re-layouts: 6.28 us -> none  [the longest x6 5.68 us: in_call(): operands = [tokens, gain[None], q_gain[None], k_gain[None], *weights]]
where the time goes in v2:
time: 258 us; the launch traced here: 257 us
  Pallas kernels  256 us (99%)
    pallas_call x2, Pallas kernels, in_call(): pl.pallas_call(functools.partial(in_kernel, span, up is not None, float(d...  145 us
    pallas_call x2, Pallas kernels, out_call(): pl.pallas_call(functools.partial(out_kernel, up is not None), name=name,...  111 us

profile of v2, /device:TPU:0, one launch (start us, length us, event | category | flops | bytes accessed | tf_op | source)
XLA Modules:
  0.0 257.5 jit_solution(2112428102744594936)
XLA Ops:
  0.0 88.2 %camera_in.1 = (bf16[2,256,384]{2,1,0:T(8,128)(2,1)}, bf16[3,2,256,512]{3,2,1,0:T(8,128)(2,1)}) custom-call(bf16[128,1536]{1,0:T(8,128)(2,1)} %refs_0_.3, f32[1536]{0:T(1024)} %refs_1_.2, f32[1536]{0:T(1024)} %refs_2_.4, f32[1536]{0:T(1024)} %refs_3_.3, bf16[1536,1536]{1,0:T(8,128)(2,1)} %refs_4_.2, bf16[1536,1536]{1,0:T(8,128)(2,1)} %refs_5_.3, ...), custom_call_target="tpu_custom_call" | custom-call | tf_op jit(solution)/shard_map/camera_in/pallas_call | solution.py:551
  88.2 67.0 %camera_out.1.refs_0_ = bf16[128,1536]{1,0:T(8,128)(2,1)} custom-call(bf16[128,1536]{1,0:T(8,128)(2,1)} %refs_0_.3, bf16[1,2,256,384]{3,2,1,0:T(8,128)(2,1)} %bitcast.4, bf16[1536,1536]{1,0:T(8,128)(2,1)} %refs_2_.5, f32[1536]{0:T(1024)} %refs_3_.4, bf16[3,2,256,512]{3,2,1,0:T(8,128)(2,1)} %get-tuple-element.8.refs_4_, bf16[6144,1536]{1,0:T(8,128)(2,1)} %refs_5_.4), custom_call_target="tpu_custom_call" | custom-call | tf_op jit(solution)/shard_map/camera_out/pallas_call | solution.py:817
  155.2 56.5 %join_in.1 = bf16[2,256,384]{2,1,0:T(8,128)(2,1)} custom-call(bf16[128,1536]{1,0:T(8,128)(2,1)} %camera_out.1.refs_0_, f32[1536]{0:T(1024)} %refs_1_.3, f32[1536]{0:T(1024)} %refs_2_.6, f32[1536]{0:T(1024)} %refs_3_.5, bf16[1536,1536]{1,0:T(8,128)(2,1)} %refs_4_.3, bf16[1536,1536]{1,0:T(8,128)(2,1)} %refs_5_.5, bf16[1536,1536]{1,0:T(8,128)(2,1)} %refs_6_.3), custom_call_target="tpu_custom_call" | custom-call | tf_op jit(solution)/shard_map/join_in/pallas_call | solution.py:551
  211.7 44.0 %join_out.1 = bf16[128,1536]{1,0:T(8,128)(2,1)} custom-call(bf16[128,1536]{1,0:T(8,128)(2,1)} %camera_out.1.refs_0_, bf16[1,2,256,384]{3,2,1,0:T(8,128)(2,1)} %bitcast.3, bf16[1536,1536]{1,0:T(8,128)(2,1)} %refs_2_.7), custom_call_target="tpu_custom_call" | custom-call | tf_op jit(solution)/shard_map/join_out/pallas_call | solution.py:817
  255.7 1.8 copy.21

commit v3 on v2

--- a/solution.py
+++ b/solution.py
@@ -333,9 +333,9 @@
     if has_up:
         out_u = refs.pop(0)
     normed, moments, m_send, m_recv, z_right, z_left, z_arrive, queries, keys, values = refs[:10]
-    groups = [refs[10:21]]
+    groups = [refs[10:25]]
     if has_up:
-        groups.append(refs[21:32])
+        groups.append(refs[25:40])
     col, mate, across = places()
     diagonal = mate + across - col
     row, row_count = lax.axis_index("rows"), lax.axis_size("rows")
@@ -393,83 +393,99 @@
         swap.wait_send()
 
     def ops(group):
-        held, p_send, p_recv, y_send, y_recv, own_sum, _, ps, pr, ys, yr = group
-
-        def product(unit, half, owner, fresh):
+        held, f_send, f_recv, p_send, p_recv, own_sum, _, y_send, y_recv, fs, fr, ps, pr, ys, yr = group
+
+        def product(unit, left, owner, fresh):
             weight = held.at[unit * 4 + owner]
             if fresh:
                 pltpu.make_async_copy(weight, weight, group[6].at[unit * 4 + owner]).wait()
-            left = normed[pl.ds(half * near, near)].reshape(near * own_rows, normed.shape[-1])
             return jnp.dot(left, weight[...], preferred_element_type=F32)
 
-        def to_mate(kind, unit, half):
+        def first_to_mate(unit, block):
             return remote(
-                p_send.at[kind, unit, half],
-                p_recv.at[kind, unit, half],
-                ps.at[kind, unit, half],
-                pr.at[kind, unit, half],
+                f_send.at[unit, block],
+                f_recv.at[unit, block],
+                fs.at[unit, block],
+                fr.at[unit, block],
                 {"cols": mate},
             )
 
-        def to_across(unit, half):
+        def second_to_mate(unit, half):
             return remote(
-                y_send.at[unit, half],
-                y_recv.at[unit, half],
-                ys.at[unit, half],
-                yr.at[unit, half],
+                p_send.at[unit, half],
+                p_recv.at[unit, half],
+                ps.at[unit, half],
+                pr.at[unit, half],
+                {"cols": mate},
+            )
+
+        def to_across(unit, block):
+            return remote(
+                y_send.at[unit, block],
+                y_recv.at[unit, block],
+                ys.at[unit, block],
+                yr.at[unit, block],
                 {"cols": across},
             )
 
-        def first(unit, half, fresh):
-            p_send[0, unit, half] = product(unit, half, diagonal, fresh).astype(BF16)
-            to_mate(0, unit, half).start()
-            partial = product(unit, half, across, fresh)
-            to_mate(0, unit, half).wait_recv()
-            y_send[unit, half] = (partial + p_recv[0, unit, half].astype(F32)).astype(BF16)
-            to_across(unit, half).start()
-
-        def second(unit, half, fresh):
-            p_send[1, unit, half] = product(unit, half, mate, fresh).astype(BF16)
-            to_mate(1, unit, half).start()
-            partial = product(unit, half, col, fresh)
-            to_mate(1, unit, half).wait_recv()
-            own_sum[unit, half] = partial + p_recv[1, unit, half].astype(F32)
+        def first(block, fresh):
+            def give(unit):
+                f_send[unit, block] = product(unit, normed[block], diagonal, fresh).astype(BF16)
+                first_to_mate(unit, block).start()
+
+            def send(unit):
+                partial = product(unit, normed[block], across, fresh)
+                first_to_mate(unit, block).wait_recv()
+                y_send[unit, block] = (partial + f_recv[unit, block].astype(F32)).astype(BF16)
+                to_across(unit, block).start()
+
+            each(own_sum.shape[0], give)
+            each(own_sum.shape[0], send)
+
+        def second(half, fresh):
+            def rows_in():
+                return normed[pl.ds(half * near, near)].reshape(near * own_rows, normed.shape[-1])
+
+            def give(unit):
+                p_send[unit, half] = product(unit, rows_in(), mate, fresh).astype(BF16)
+                second_to_mate(unit, half).start()
+
+            def keep(unit):
+                partial = product(unit, rows_in(), col, fresh)
+                second_to_mate(unit, half).wait_recv()
+                own_sum[unit, half] = partial + p_recv[unit, half].astype(F32)
+
+            each(own_sum.shape[0], give)
+            each(own_sum.shape[0], keep)
 
         def final(unit, half):
-            to_across(unit, half).wait_recv()
-            return own_sum[unit, half] + y_recv[unit, half].astype(F32)
+            for place in range(near):
+                to_across(unit, half * near + place).wait_recv()
+            arrived = y_recv[unit, pl.ds(half * near, near)].astype(F32)
+            return own_sum[unit, half] + arrived.reshape(near * own_rows, -1)
 
         def finish(unit):
+            for block in range(row_count):
+                first_to_mate(unit, block).wait_send()
+                to_across(unit, block).wait_send()
             for half in range(2):
-                to_mate(0, unit, half).wait_send()
-                to_mate(1, unit, half).wait_send()
-                to_across(unit, half).wait_send()
+                second_to_mate(unit, half).wait_send()
 
         return first, second, final, finish, own_sum.shape[0]
 
     all_ops = [ops(group) for group in groups]
-    for away in range(1, near):
-        take_rows(away)
     home = row // near
-    for half, fresh in ((home, True), (1 - home, False)):
-        for first, second, final, finish, count in all_ops:
-            each(count, lambda unit: first(unit, half, fresh))
-        if fresh:
-            for away in range(near, row_count - 1):
-                take_rows(away)
-        for first, second, final, finish, count in all_ops:
-            each(count, lambda unit: second(unit, half, fresh))
-        if fresh:
-            take_rows(row_count - 1)
-    final = all_ops[0][2]
     wide = groups[0][0].shape[-1]
     mine = pl.ds(pl.multiple_of(col * wide, HEAD_DIM), wide)
     half_rows = near * own_rows
-    for half in range(2):
-        rows = slice(half * half_rows, (half + 1) * half_rows)
-        queries[rows] = norm_heads(final(0, half), q_gain[mine].reshape(1, -1))
-        keys[rows] = norm_heads(final(1, half), k_gain[mine].reshape(1, -1))
-        values[rows] = final(2, half).astype(BF16)
+
+    def firsts(block, fresh):
+        for first, *_ in all_ops:
+            first(block, fresh)
+
+    def seconds(half, fresh):
+        for _, second, *_ in all_ops:
+            second(half, fresh)
 
     def camera(which):
         rows = pl.ds(pl.multiple_of(which * span, span), span)
@@ -486,19 +502,41 @@
             rows = pl.ds(pl.multiple_of(half * half_rows, half_rows), half_rows)
             out_a[half, :, head] = soft_blend(queries[rows, head], keys[:, head], values[:, head])
 
+    def finals(half):
+        final = all_ops[0][2]
+        rows = pl.ds(pl.multiple_of(half * half_rows, half_rows), half_rows)
+        queries[rows] = norm_heads(final(0, half), q_gain[mine].reshape(1, -1))
+        keys[rows] = norm_heads(final(1, half), k_gain[mine].reshape(1, -1))
+        values[rows] = final(2, half).astype(BF16)
+        if span < half_rows:
+            count = half_rows // span
+            each(count, lambda which: camera(half * count + which))
+        if has_up:
+            up_final = all_ops[1][2]
+
+            def activate(unit):
+                raw = up_final(unit, half) + bias[col * out_u.shape[0] + unit]
+                out_u[unit, half] = (raw * (1.0 + lax.erf(raw * math.sqrt(0.5))) * 0.5).astype(BF16)
+
+            each(out_u.shape[0], activate)
+
+    firsts(row, True)
+    take_rows(1)
+    firsts(row + 1 - 2 * lax.rem(row, 2), False)
+    seconds(home, True)
+    take_rows(2)
+    firsts(near - home, False)
+    take_rows(3)
+    firsts((row_count - 1) * (1 - home), False)
+    if has_up:
+        finals(home)
+        seconds(1 - home, False)
+    else:
+        seconds(1 - home, False)
+        finals(home)
+    finals(1 - home)
     if span == 2 * half_rows:
         each(2, joint)
-    else:
-        each(2 * half_rows // span, camera)
-    if has_up:
-        final = all_ops[1][2]
-
-        def activate(unit):
-            for half in range(2):
-                raw = final(unit, half) + bias[col * out_u.shape[0] + unit]
-                out_u[unit, half] = (raw * (1.0 + lax.erf(raw * math.sqrt(0.5))) * 0.5).astype(BF16)
-
-        each(out_u.shape[0], activate)
     for first, second, final, finish, count in all_ops:
         each(count, finish)
     finish_rows()
@@ -537,16 +575,20 @@
     for count, piece in groups:
         scratch += [
             pltpu.VMEM((count * 4, depth, piece), BF16),
-            pltpu.VMEM((2, count, 2, half_rows, piece), BF16),
-            pltpu.VMEM((2, count, 2, half_rows, piece), BF16),
+            pltpu.VMEM((count, row_count, own_rows, piece), BF16),
+            pltpu.VMEM((count, row_count, own_rows, piece), BF16),
             pltpu.VMEM((count, 2, half_rows, piece), BF16),
             pltpu.VMEM((count, 2, half_rows, piece), BF16),
             pltpu.VMEM((count, 2, half_rows, piece), F32),
             dma((count * 4,)),
-            dma((2, count, 2)),
-            dma((2, count, 2)),
+            pltpu.VMEM((count, row_count, own_rows, piece), BF16),
+            pltpu.VMEM((count, row_count, own_rows, piece), BF16),
+            dma((count, row_count)),
+            dma((count, row_count)),
             dma((count, 2)),
             dma((count, 2)),
+            dma((count, row_count)),
+            dma((count, row_count)),
         ]
     return pl.pallas_call(
         functools.partial(in_kernel, span, up is not None, float(depth * cols)),
@@ -598,34 +640,40 @@
             each(group[0].shape[0] // 4, lambda unit: load(group_id, unit, place).start())
     greet(2)
 
+    def part_of(ref, stage):
+        return ref.at[pl.ds(stage[0], stage[1])]
+
+    def read(ref, stage):
+        return part_of(ref, stage)[...].reshape(stage[1] * own_rows, -1)
+
     def copies(group_id):
         _, _, got, y_send, p_send, f_send, y_recv, p_recv = groups[group_id]
         source = sources[group_id][0]
 
         def to_across(unit, half):
             return remote(
-                source.at[unit, half],
-                got.at[1, unit, half],
-                y_send.at[unit, half],
-                y_recv.at[unit, half],
+                part_of(source.at[unit], half),
+                part_of(got.at[1, unit], half),
+                y_send.at[unit, half[2]],
+                y_recv.at[unit, half[2]],
                 {"cols": across},
             )
 
         def to_mate(unit, half):
             return remote(
-                source.at[unit, half],
-                got.at[0, unit, half],
-                p_send.at[unit, half],
-                p_recv.at[0, unit, half],
+                part_of(source.at[unit], half),
+                part_of(got.at[0, unit], half),
+                p_send.at[unit, half[2]],
+                p_recv.at[0, unit, half[2]],
                 {"cols": mate},
             )
 
         def forward(unit, half):
             return remote(
-                got.at[1, unit, half],
-                got.at[2, unit, half],
-                f_send.at[unit, half],
-                p_recv.at[1, unit, half],
+                part_of(got.at[1, unit], half),
+                part_of(got.at[2, unit], half),
+                f_send.at[unit, half[2]],
+                p_recv.at[1, unit, half[2]],
                 {"cols": mate},
             )
 
@@ -633,8 +681,9 @@
 
     moves = [copies(group_id) for group_id in range(len(groups))]
     home = row // near
-    halves = ((1 - home, True), (home, False))
-    for half, _ in halves:
+    pair = row + 1 - 2 * lax.rem(row, 2)
+    stages = (((1 - home) * near, near, 0), (pair, 1, 1), (row, 1, 2))
+    for half in stages:
         for to_across, to_mate, forward, count in moves:
             each(count, lambda unit: to_across(unit, half).start())
             each(count, lambda unit: to_mate(unit, half).start())
@@ -645,22 +694,23 @@
         held = groups[group_id][0]
         count = held.shape[0] // 4
         part = jnp.dot(piece, held[place * count + unit], preferred_element_type=F32)
+        part = part.reshape(half[1], own_rows, -1)
         if begin:
-            accum[half] = part
+            part_of(accum, half)[...] = part
         else:
-            accum[half] += part
+            part_of(accum, half)[...] += part
 
     def near_chunks(half, fresh):
         for group_id, (to_across, to_mate, forward, count) in enumerate(moves):
             source, got = sources[group_id][0], groups[group_id][2]
             if group_id == 0:
-                add(0, 0, 0, half, fresh, source[0, half], True)
+                add(0, 0, 0, half, fresh, read(source.at[0], half), True)
             else:
-                each(count, lambda unit: add(group_id, unit, 0, half, fresh, source[unit, half]))
+                each(count, lambda unit: add(group_id, unit, 0, half, fresh, read(source.at[unit], half)))
 
             def from_mate(unit):
                 to_mate(unit, half).wait_recv()
-                add(group_id, unit, 1, half, fresh, got[0, unit, half])
+                add(group_id, unit, 1, half, fresh, read(got.at[0, unit], half))
 
             each(count, from_mate)
 
@@ -671,115 +721,128 @@
             def from_across(unit):
                 to_across(unit, half).wait_recv()
                 forward(unit, half).start()
-                add(group_id, unit, 2, half, fresh, got[1, unit, half])
+                add(group_id, unit, 2, half, fresh, read(got.at[1, unit], half))
                 forward(unit, half).wait_recv()
-                add(group_id, unit, 3, half, fresh, got[2, unit, half])
+                add(group_id, unit, 3, half, fresh, read(got.at[2, unit], half))
 
             each(count, from_across)
 
-    def rows_of(block):
-        return accum[block // near, (block % near) * own_rows : (block % near + 1) * own_rows]
-
-    def to_right(block):
+    piece_wide = from_left.shape[-1]
+    pieces = from_left.shape[1]
+
+    def term(block, piece):
+        return accum[block, :, piece * piece_wide : (piece + 1) * piece_wide]
+
+    def to_right(block, piece):
         return remote(
-            right_send.at[block], from_left.at[block], r_send.at[block], r_recv.at[block], {"rows": row + 1}
+            right_send.at[block, piece],
+            from_left.at[block, piece],
+            r_send.at[block, piece],
+            r_recv.at[block, piece],
+            {"rows": row + 1},
         )
 
-    def to_left(block):
+    def to_left(block, piece):
         return remote(
-            left_send.at[block], from_right.at[block], l_send.at[block], l_recv.at[block], {"rows": row - 1}
+            left_send.at[block, piece],
+            from_right.at[block, piece],
+            l_send.at[block, piece],
+            l_recv.at[block, piece],
+            {"rows": row - 1},
         )
 
+    def run(move, send, arrived, block, edge):
+        for piece in range(pieces):
+
+            @pl.when(row == edge)
+            def _():
+                send[block, piece] = term(block, piece).astype(BF16)
+
+            @pl.when(row != edge)
+            def _():
+                move(block, piece).wait_recv()
+                send[block, piece] = (
+                    term(block, piece) + arrived[block, piece].astype(F32)
+                ).astype(BF16)
+
+            move(block, piece).start()
+
     def run_right(block):
-        @pl.when((row < block) & (row == 0))
-        def _():
-            right_send[block] = rows_of(block).astype(BF16)
-
-        @pl.when((row < block) & (row > 0))
-        def _():
-            to_right(block).wait_recv()
-            right_send[block] = (rows_of(block) + from_left[block].astype(F32)).astype(BF16)
-
-        @pl.when(row < block)
-        def _():
-            to_right(block).start()
+        run(to_right, right_send, from_left, block, 0)
 
     def run_left(block):
-        @pl.when((row > block) & (row == row_count - 1))
-        def _():
-            left_send[block] = rows_of(block).astype(BF16)
-
-        @pl.when((row > block) & (row < row_count - 1))
-        def _():
-            to_left(block).wait_recv()
-            left_send[block] = (rows_of(block) + from_right[block].astype(F32)).astype(BF16)
-
-        @pl.when(row > block)
-        def _():
-            to_left(block).start()
+        run(to_left, left_send, from_right, block, row_count - 1)
 
     def send_far(from_end):
         at_end = (row == 0) | (row == row_count - 1)
         now = at_end if from_end else jnp.logical_not(at_end)
-        for step in range(near):
-
-            @pl.when(now & (row < near))
+
+        @pl.when(now & (row < near))
+        def _():
+            each(near, lambda step: run_right(row_count - 1 - step))
+
+        @pl.when(now & (row >= near))
+        def _():
+            each(near, run_left)
+
+    near_chunks(stages[0], True)
+    far_chunks(stages[0], True)
+    send_far(True)
+    near_chunks(stages[1], False)
+    if has_up:
+        far_chunks(stages[1], False)
+        send_far(False)
+        near_chunks(stages[2], False)
+    else:
+        far_chunks(stages[1], False)
+        near_chunks(stages[2], False)
+        send_far(False)
+
+    @pl.when(row < pair)
+    def _():
+        run_right(pair)
+
+    @pl.when(row > pair)
+    def _():
+        run_left(pair)
+
+    far_chunks(stages[2], False)
+    for piece in range(pieces):
+        columns = slice(piece * piece_wide, (piece + 1) * piece_wide)
+        total = term(row, piece) + base[:, columns].astype(F32)
+        if has_up:
+            total += bias[columns].reshape(1, -1)
+        accum[row, :, columns] = total
+
+        @pl.when(row > 0)
+        def _():
+            to_right(row, piece).wait_recv()
+            accum[row, :, columns] += from_left[row, piece].astype(F32)
+
+        @pl.when(row < row_count - 1)
+        def _():
+            to_left(row, piece).wait_recv()
+            accum[row, :, columns] += from_right[row, piece].astype(F32)
+
+        result[:, columns] = term(row, piece).astype(BF16)
+
+    def sent(block):
+        for piece in range(pieces):
+
+            @pl.when(row < block)
             def _():
-                run_right(row_count - 1 - step)
-
-            @pl.when(now & (row >= near))
+                to_right(block, piece).wait_send()
+
+            @pl.when(row > block)
             def _():
-                run_left(step)
-
-    near_chunks(*halves[0])
-    far_chunks(*halves[0])
-    send_far(True)
-    near_chunks(*halves[1])
-    send_far(False)
-    far_chunks(*halves[1])
-    for step in range(row_count - 1):
-        block = row_count - 1 - step
-
-        @pl.when(home == block // near)
-        def _():
-            run_right(block)
-
-    for block in range(row_count - 1):
-
-        @pl.when(home == block // near)
-        def _():
-            run_left(block)
-
-    for block in range(row_count):
-
-        @pl.when(row == block)
-        def _():
-            total = rows_of(block)
-            if block > 0:
-                to_right(block).wait_recv()
-                total += from_left[block].astype(F32)
-            if block < row_count - 1:
-                to_left(block).wait_recv()
-                total += from_right[block].astype(F32)
-            total += base[...].astype(F32)
-            if has_up:
-                total += bias[...].reshape(1, -1)
-            result[...] = total.astype(BF16)
-
-    for block in range(row_count):
-
-        @pl.when(row < block)
-        def _():
-            to_right(block).wait_send()
-
-        @pl.when(row > block)
-        def _():
-            to_left(block).wait_send()
+                to_left(block, piece).wait_send()
+
+    each(row_count, sent)
 
     for to_across, to_mate, forward, count in moves:
 
         def finish(unit):
-            for half in range(2):
+            for half in stages:
                 to_across(unit, half).wait_send()
                 to_mate(unit, half).wait_send()
                 forward(unit, half).wait_send()
@@ -792,27 +855,30 @@
     _, half_rows, wide = heads.shape
     row_count = lax.axis_size("rows")
     any_spec, vmem_spec = pl.BlockSpec(memory_space=pl.ANY), pl.BlockSpec(memory_space=pltpu.VMEM)
-    operands = [base, heads[None], w_out]
+    row_count = lax.axis_size("rows")
+    operands = [base, heads.reshape(1, row_count, own_rows, wide), w_out]
     in_specs = [vmem_spec, vmem_spec, any_spec]
     groups = [(1, wide)]
     if up is not None:
         bias, hidden, w_down = up
-        operands += [bias, hidden, w_down]
+        operands += [bias, hidden.reshape(hidden.shape[0], row_count, own_rows, -1), w_down]
         in_specs += [vmem_spec, vmem_spec, any_spec]
         groups.append((hidden.shape[0], hidden.shape[3]))
     dma = pltpu.SemaphoreType.DMA
-    block = pltpu.VMEM((row_count, own_rows, width), BF16)
-    scratch = [pltpu.VMEM((2, half_rows, width), F32)] + [block] * 4 + [dma((row_count,))] * 4
+    piece_wide = up_tile(width)
+    pieces = width // piece_wide
+    block = pltpu.VMEM((row_count, pieces, own_rows, piece_wide), BF16)
+    scratch = [pltpu.VMEM((row_count, own_rows, width), F32)] + [block] * 4 + [dma((row_count, pieces))] * 4
     for count, piece in groups:
         scratch += [
             pltpu.VMEM((4 * count, piece, width), BF16),
             dma((4 * count,)),
-            pltpu.VMEM((3, count, 2, half_rows, piece), BF16),
-            dma((count, 2)),
-            dma((count, 2)),
-            dma((count, 2)),
-            dma((count, 2)),
-            dma((2, count, 2)),
+            pltpu.VMEM((3, count, row_count, own_rows, piece), BF16),
+            dma((count, 3)),
+            dma((count, 3)),
+            dma((count, 3)),
+            dma((count, 3)),
+            dma((2, count, 3)),
         ]
     return pl.pallas_call(
         functools.partial(out_kernel, up is not None),
@@ -885,7 +951,7 @@
 
 def fits(mesh):
     cols, rows = mesh.shape["cols"], mesh.shape["rows"]
-    return cols == 4 and rows > 2 and rows % 2 == 0 and D % (rows * cols * HEAD_DIM) == 0
+    return cols == 4 and rows == 4 and D % (rows * cols * HEAD_DIM) == 0
 
 
 def solution(mesh):

time: 258 us -> 233 us (0.903)
  Pallas kernels: 256 us -> 231 us
    pallas_call x2, Pallas kernels: 145 us -> 126 us  [in_call(): pl.pallas_call(functools.partial(in_kernel, span, up is not None, float(d...]
    pallas_call x2, Pallas kernels: 111 us -> 105 us  [out_call(): pl.pallas_call(functools.partial(out_kernel, up is not None), name=name,...]
where the time goes in v3:
time: 233 us
  Pallas kernels  231 us (99%)
    pallas_call x2, Pallas kernels, in_call(): pl.pallas_call(functools.partial(in_kernel, span, up is not None, float(d...  126 us
    pallas_call x2, Pallas kernels, out_call(): pl.pallas_call(functools.partial(out_kernel, up is not None), name=name,...  105 us

profile of v3, /device:TPU:0, one launch (start us, length us, event | category | flops | bytes accessed | tf_op | source)
XLA Modules:
  0.0 232.7 jit_solution(9902194055830135861)
XLA Ops:
  0.0 74.7 %camera_in.1 = (bf16[2,256,384]{2,1,0:T(8,128)(2,1)}, bf16[3,2,256,512]{3,2,1,0:T(8,128)(2,1)}) custom-call(bf16[128,1536]{1,0:T(8,128)(2,1)} %refs_0_.3, f32[1536]{0:T(1024)} %refs_1_.2, f32[1536]{0:T(1024)} %refs_2_.4, f32[1536]{0:T(1024)} %refs_3_.3, bf16[1536,1536]{1,0:T(8,128)(2,1)} %refs_4_.2, bf16[1536,1536]{1,0:T(8,128)(2,1)} %refs_5_.3, ...), custom_call_target="tpu_custom_call" | custom-call | tf_op jit(solution)/shard_map/camera_in/pallas_call | solution.py:593
  74.7 62.9 %camera_out.1.refs_0_ = bf16[128,1536]{1,0:T(8,128)(2,1)} custom-call(bf16[128,1536]{1,0:T(8,128)(2,1)} %refs_0_.3, bf16[1,4,128,384]{3,2,1,0:T(8,128)(2,1)} %bitcast.6, bf16[1536,1536]{1,0:T(8,128)(2,1)} %refs_2_.5, f32[1536]{0:T(1024)} %refs_3_.4, bf16[3,4,128,512]{3,2,1,0:T(8,128)(2,1)} %bitcast.4, bf16[6144,1536]{1,0:T(8,128)(2,1)} %refs_5_.4), custom_call_target="tpu_custom_call" | custom-call | tf_op jit(solution)/shard_map/camera_out/pallas_call | solution.py:883
  137.6 51.6 %join_in.1 = bf16[2,256,384]{2,1,0:T(8,128)(2,1)} custom-call(bf16[128,1536]{1,0:T(8,128)(2,1)} %camera_out.1.refs_0_, f32[1536]{0:T(1024)} %refs_1_.3, f32[1536]{0:T(1024)} %refs_2_.6, f32[1536]{0:T(1024)} %refs_3_.5, bf16[1536,1536]{1,0:T(8,128)(2,1)} %refs_4_.3, bf16[1536,1536]{1,0:T(8,128)(2,1)} %refs_5_.5, bf16[1536,1536]{1,0:T(8,128)(2,1)} %refs_6_.3), custom_call_target="tpu_custom_call" | custom-call | tf_op jit(solution)/shard_map/join_in/pallas_call | solution.py:593
  189.3 41.6 %join_out.1 = bf16[128,1536]{1,0:T(8,128)(2,1)} custom-call(bf16[128,1536]{1,0:T(8,128)(2,1)} %camera_out.1.refs_0_, bf16[1,4,128,384]{3,2,1,0:T(8,128)(2,1)} %bitcast.5, bf16[1536,1536]{1,0:T(8,128)(2,1)} %refs_2_.7), custom_call_target="tpu_custom_call" | custom-call | tf_op jit(solution)/shard_map/join_out/pallas_call | solution.py:883
  230.9 1.8 copy.21

commit v4 on v3

--- a/solution.py
+++ b/solution.py
@@ -322,7 +322,7 @@
     return (blended / total).astype(BF16)
 
 
-def in_kernel(span, has_up, width, *refs):
+def in_kernel(span, has_up, width, *refs, follow=None):
     refs = list(refs)
     tokens, gain, q_gain, k_gain, wq, wk, wv = refs[:7]
     refs = refs[7:]
@@ -500,7 +500,8 @@
         for start in range(0, wide, HEAD_DIM):
             head = slice(start, start + HEAD_DIM)
             rows = pl.ds(pl.multiple_of(half * half_rows, half_rows), half_rows)
-            out_a[half, :, head] = soft_blend(queries[rows, head], keys[:, head], values[:, head])
+            blended = soft_blend(queries[rows, head], keys[:, head], values[:, head])
+            out_a[0, pl.ds(half * near, near), :, head] = blended.reshape(near, own_rows, HEAD_DIM)
 
     def finals(half):
         final = all_ops[0][2]
@@ -535,14 +536,14 @@
         seconds(1 - home, False)
         finals(home)
     finals(1 - home)
-    if span == 2 * half_rows:
-        each(2, joint)
+    if follow is not None:
+        follow(joint)
     for first, second, final, finish, count in all_ops:
         each(count, finish)
     finish_rows()
 
 
-def in_call(name, number, span, tokens, gain, q_gain, k_gain, weights, up=None):
+def in_call(name, number, span, tokens, gain, q_gain, k_gain, weights, up=None, join=None):
     own_rows, depth = tokens.shape
     all_rows = own_rows * lax.axis_size("rows")
     cols = lax.axis_size("cols")
@@ -590,6 +591,19 @@
             dma((count, row_count)),
             dma((count, row_count)),
         ]
+    if join is not None:
+        base_scratch = out_scratch([(1, wide)], own_rows, join.shape[1], row_count)
+        return pl.pallas_call(
+            functools.partial(join_kernel, span, float(depth * cols)),
+            name=name,
+            out_shape=jax.ShapeDtypeStruct((own_rows, join.shape[1]), BF16),
+            in_specs=in_specs + [any_spec],
+            out_specs=vmem_spec,
+            scratch_shapes=[pltpu.VMEM((1, row_count, own_rows, wide), BF16)] + scratch + base_scratch,
+            compiler_params=pltpu.CompilerParams(
+                collective_id=number, has_side_effects=True, vmem_limit_bytes=VMEM_LIMIT
+            ),
+        )(*operands, join)
     return pl.pallas_call(
         functools.partial(in_kernel, span, up is not None, float(depth * cols)),
         name=name,
@@ -604,6 +618,26 @@
 
 
 def out_kernel(has_up, *refs):
+    for _ in out_steps(has_up, {}, *refs):
+        pass
+
+
+def join_kernel(span, width, tokens, gain, q_gain, k_gain, wq, wk, wv, w_out, result, heads, *rest):
+    later = {}
+    steps = out_steps(False, later, tokens, heads, w_out, result, *rest[25:])
+    next(steps)
+
+    def follow(joint):
+        later["joint"] = joint
+        for _ in steps:
+            pass
+
+    in_kernel(
+        span, False, width, tokens, gain, q_gain, k_gain, wq, wk, wv, heads, *rest[:25], follow=follow
+    )
+
+
+def out_steps(has_up, later, *refs):
     refs = list(refs)
     base, heads, w_out = refs[:3]
     refs = refs[3:]
@@ -638,7 +672,10 @@
     for place in range(4):
         for group_id, group in enumerate(groups):
             each(group[0].shape[0] // 4, lambda unit: load(group_id, unit, place).start())
-    greet(2)
+    yield
+    joint = later.get("joint")
+    if joint is None:
+        greet(2)
 
     def part_of(ref, stage):
         return ref.at[pl.ds(stage[0], stage[1])]
@@ -683,10 +720,18 @@
     home = row // near
     pair = row + 1 - 2 * lax.rem(row, 2)
     stages = (((1 - home) * near, near, 0), (pair, 1, 1), (row, 1, 2))
-    for half in stages:
+
+    def share(half):
         for to_across, to_mate, forward, count in moves:
             each(count, lambda unit: to_across(unit, half).start())
             each(count, lambda unit: to_mate(unit, half).start())
+
+    if joint is not None:
+        joint(1 - home)
+    share(stages[0])
+    if joint is None:
+        share(stages[1])
+        share(stages[2])
 
     def add(group_id, unit, place, half, fresh, piece, begin=False):
         if fresh:
@@ -788,6 +833,10 @@
     near_chunks(stages[0], True)
     far_chunks(stages[0], True)
     send_far(True)
+    if joint is not None:
+        joint(home)
+        share(stages[1])
+        share(stages[2])
     near_chunks(stages[1], False)
     if has_up:
         far_chunks(stages[1], False)
@@ -850,20 +899,7 @@
         each(count, finish)
 
 
-def out_call(name, number, base, heads, w_out, up=None):
-    own_rows, width = base.shape
-    _, half_rows, wide = heads.shape
-    row_count = lax.axis_size("rows")
-    any_spec, vmem_spec = pl.BlockSpec(memory_space=pl.ANY), pl.BlockSpec(memory_space=pltpu.VMEM)
-    row_count = lax.axis_size("rows")
-    operands = [base, heads.reshape(1, row_count, own_rows, wide), w_out]
-    in_specs = [vmem_spec, vmem_spec, any_spec]
-    groups = [(1, wide)]
-    if up is not None:
-        bias, hidden, w_down = up
-        operands += [bias, hidden.reshape(hidden.shape[0], row_count, own_rows, -1), w_down]
-        in_specs += [vmem_spec, vmem_spec, any_spec]
-        groups.append((hidden.shape[0], hidden.shape[3]))
+def out_scratch(groups, own_rows, width, row_count):
     dma = pltpu.SemaphoreType.DMA
     piece_wide = up_tile(width)
     pieces = width // piece_wide
@@ -880,6 +916,24 @@
             dma((count, 3)),
             dma((2, count, 3)),
         ]
+    return scratch
+
+
+def out_call(name, number, base, heads, w_out, up=None):
+    own_rows, width = base.shape
+    _, half_rows, wide = heads.shape
+    row_count = lax.axis_size("rows")
+    any_spec, vmem_spec = pl.BlockSpec(memory_space=pl.ANY), pl.BlockSpec(memory_space=pltpu.VMEM)
+    row_count = lax.axis_size("rows")
+    operands = [base, heads.reshape(1, row_count, own_rows, wide), w_out]
+    in_specs = [vmem_spec, vmem_spec, any_spec]
+    groups = [(1, wide)]
+    if up is not None:
+        bias, hidden, w_down = up
+        operands += [bias, hidden.reshape(hidden.shape[0], row_count, own_rows, -1), w_down]
+        in_specs += [vmem_spec, vmem_spec, any_spec]
+        groups.append((hidden.shape[0], hidden.shape[3]))
+    scratch = out_scratch(groups, own_rows, width, row_count)
     return pl.pallas_call(
         functools.partial(out_kernel, up is not None),
         name=name,
@@ -936,8 +990,8 @@
     layer_own = out_call(
         "camera_out", 1, camera_tokens, heads, out_weight, (down_bias, hidden, down_weight)
     )
-    (joined,) = in_call(
-        "join_in",
+    return in_call(
+        "join",
         2,
         all_rows,
         layer_own,
@@ -945,8 +999,8 @@
         join_query_gain,
         join_key_gain,
         (join_query, join_key, join_value),
-    )
-    return out_call("join_out", 3, layer_own, joined, join_out)
+        join=join_out,
+    )
 
 
 def fits(mesh):

time: 233 us -> 229 us (0.983)
  Pallas kernels: 231 us -> 227 us
    pallas_call x0 -> x1, Pallas kernels: none -> 89 us  [in_call(): pl.pallas_call(functools.partial(join_kernel, span, float(depth * cols)),...]
    pallas_call x2 -> x1, Pallas kernels: 126 us -> 74.7 us  [in_call(): pl.pallas_call(functools.partial(in_kernel, span, up is not None, float(d...]
    pallas_call x2 -> x1, Pallas kernels: 105 us -> 62.9 us  [out_call(): pl.pallas_call(functools.partial(out_kernel, up is not None), name=name,...]
where the time goes in v4:
time: 229 us; the launch traced here: 228 us
  Pallas kernels  227 us (99%)
    pallas_call x1, Pallas kernels, in_call(): pl.pallas_call(functools.partial(join_kernel, span, float(depth * cols)),...  89 us
    pallas_call x1, Pallas kernels, in_call(): pl.pallas_call(functools.partial(in_kernel, span, up is not None, float(d...  74.7 us
    pallas_call x1, Pallas kernels, out_call(): pl.pallas_call(functools.partial(out_kernel, up is not None), name=name,...  62.9 us

profile of v4, /device:TPU:0, one launch (start us, length us, event | category | flops | bytes accessed | tf_op | source)
XLA Modules:
  0.0 228.3 jit_solution(3661045645240443519)
XLA Ops:
  0.0 74.7 %camera_in.1 = (bf16[2,256,384]{2,1,0:T(8,128)(2,1)}, bf16[3,2,256,512]{3,2,1,0:T(8,128)(2,1)}) custom-call(bf16[128,1536]{1,0:T(8,128)(2,1)} %refs_0_.3, f32[1536]{0:T(1024)} %refs_1_.1, f32[1536]{0:T(1024)} %refs_2_.2, f32[1536]{0:T(1024)} %refs_3_.2, bf16[1536,1536]{1,0:T(8,128)(2,1)} %refs_4_.1, bf16[1536,1536]{1,0:T(8,128)(2,1)} %refs_5_.2, ...), custom_call_target="tpu_custom_call" | custom-call | tf_op jit(solution)/shard_map/camera_in/pallas_call | solution.py:607
  74.7 62.9 %camera_out.1.tokens = bf16[128,1536]{1,0:T(8,128)(2,1)} custom-call(bf16[128,1536]{1,0:T(8,128)(2,1)} %refs_0_.3, bf16[1,4,128,384]{3,2,1,0:T(8,128)(2,1)} %bitcast.4, bf16[1536,1536]{1,0:T(8,128)(2,1)} %refs_2_.3, f32[1536]{0:T(1024)} %refs_3_.3, bf16[3,4,128,512]{3,2,1,0:T(8,128)(2,1)} %bitcast.3, bf16[6144,1536]{1,0:T(8,128)(2,1)} %refs_5_.3), custom_call_target="tpu_custom_call" | custom-call | tf_op jit(solution)/shard_map/camera_out/pallas_call | solution.py:937
  137.6 89.0 %join.1 = bf16[128,1536]{1,0:T(8,128)(2,1)} custom-call(bf16[128,1536]{1,0:T(8,128)(2,1)} %camera_out.1.tokens, f32[1536]{0:T(1024)} %gain.1, f32[1536]{0:T(1024)} %q_gain.1, f32[1536]{0:T(1024)} %k_gain.1, bf16[1536,1536]{1,0:T(8,128)(2,1)} %wq.1, bf16[1536,1536]{1,0:T(8,128)(2,1)} %wk.1, bf16[1536,1536]{1,0:T(8,128)(2,1)} %wv.1, bf16[1536,1536]{1,0:T(8,128)(2,1)} %w_out.1), custom_call_target="tpu_custom_call" | custom-call | tf_op jit(solution)/shard_map/join/pallas_call | solution.py:596
  226.6 1.8 copy.21
